TPU v7x, 32 devices: a whole 2x2x4 slice. The times are simulated.
32 devices in a mesh: row: 2 (over y), col: 4 (over z), layer: 4 (over x, core).
Axes of the slice: x: 2, y: 2, z: 4, core: 2. Of those that a mesh axis runs over, the one named last changes fastest.
Arguments:
- integrals: bfloat16 [64, 1024, 768], P('layer', 'col', 'row'), may hold values from -0.0234375 to 0.0234375
- amplitudes: bfloat16 [64, 1024, 512], P('layer', 'row', 'col'), may hold values from -6 to 6
- coulomb: bfloat16 [768, 512], P(('row', 'layer'), 'col'), may hold values from -6 to 6
- row_gap: float32 [768], P(('row', 'layer')), may hold values from 0.5 to 4
- col_gap: float32 [512], P('col'), may hold values from 0.5 to 4
Outputs:
- residual: float32 [768, 512], P(('row', 'layer'), 'col')
All inputs are finite; a program needn't handle non-finite values.
Results may differ from a plain program's by a relative error of at most 0.0003.
Values may be sent and summed in bfloat16 or wider, within the bound.
A program may use at most 64 MiB of HBM per device.

v0:
```python
import functools

import jax
import jax.numpy as jnp
from jax import lax
from jax.experimental import pallas as pl
from jax.experimental.pallas import tpu as pltpu
from jax.sharding import PartitionSpec as P

MESH = pl.DeviceIdType.MESH


def hi_order(n):
    if n == 1:
        return [0]
    below = hi_order(n // 2)
    return [2 * x + 1 for x in below] + [2 * x for x in below]


def kernel(R, C, L, Q, i_ref, a_ref, o_ref,
           a_all, az, i_all, i_t, acc, lay_buf, row_buf, col_buf,
           asend, arecv, xsend, xrecv, zsend, zrecv,
           osend, orecv, lsend, lrecv, rsend, rrecv, csend, crecv):
    r, c, l = lax.axis_index("row"), lax.axis_index("col"), lax.axis_index("layer")
    K, V_row, N = a_ref.shape
    V, M = i_ref.shape[1:]
    Kr = K // R
    kc = Kr // Q
    m = C // R
    w = kc * V
    rows = M // L
    stages = L.bit_length() - 1
    late = M // 2 // 128 * 128 if stages == 2 and M % 128 == 0 else 0
    early = M - late
    top = l >> (stages - 1)

    def remote(src, dst, ss, rs, **to):
        where = {"row": r, "col": c, "layer": l}
        where.update(to)
        return pltpu.make_async_remote_copy(src_ref=src, dst_ref=dst, send_sem=ss, recv_sem=rs,
                                            device_id=where, device_id_type=MESH)

    def ks(q):
        return pl.ds(q * kc, kc)

    def far_row(d):
        return lax.rem(r + d, R)

    def near(dc):
        return lax.rem(c + dc + C, C)

    order = sorted(range(1, C), key=lambda d: -min(d, C - d))

    def slice_for(d, q):
        return pl.ds(far_row(d) * Kr + q * kc, kc)

    def own_a(q):
        return pltpu.make_async_copy(a_ref.at[slice_for(0, q)], a_all.at[0, ks(q)], arecv.at[0, q])

    def own_i(q):
        return pltpu.make_async_copy(i_ref.at[slice_for(0, q)], i_all.at[0, ks(q)], xrecv.at[0, q])

    for q in range(Q):
        own_a(q).start()
        own_i(q).start()

    barrier = pltpu.get_barrier_semaphore()
    partners = [{"row": far_row(d), "col": near(dc)} for d in range(R) for dc in range(C) if d or dc]
    partners += [{"layer": l ^ (1 << t)} for t in range(stages)]
    for p in partners:
        where = {"row": r, "col": c, "layer": l}
        where.update(p)
        pl.semaphore_signal(barrier, inc=1, device_id=where, device_id_type=MESH)
    pl.semaphore_wait(barrier, len(partners))

    def row_a(d, q):
        return remote(a_ref.at[slice_for(d, q)], a_all.at[R - d, ks(q)], asend.at[d, q], arecv.at[R - d, q], row=far_row(d))

    parts = [(0, early, (1 - top) * late)] + ([(early, late, top * early)] if late else [])

    def row_i(d, q, p):
        at, size, start = parts[p]
        src = i_ref.at[slice_for(d, q), :, pl.ds(pl.multiple_of(start, 128), size)] if late else i_ref.at[slice_for(d, q)]
        return remote(src, i_all.at[R - d, ks(q), :, pl.ds(at, size)], xsend.at[p * R + d, q], xrecv.at[p * R + R - d, q],
                      row=far_row(d))

    def col_a(d, j, q):
        b = far_row(d) * m + j
        at = pl.ds(j * V, V)
        src = a_all.at[d, ks(q), at] if d else a_ref.at[slice_for(0, q), at]
        return b, remote(src, az.at[c, ks(q)], zsend.at[d, j, q], zrecv.at[c, q], col=b)

    def col_start(d, q):
        for j in range(m):
            b, cp = col_a(d, j, q)

            @pl.when(b != c)
            def _():
                cp.start()

    for q in range(Q):
        for d in range(1, R):
            row_a(d, q).start()
        col_start(0, q)
    for p in range(len(parts)):
        for q in range(Q):
            for d in range(1, R):
                row_i(d, q, p).start()

    whole = (0, M, 0)

    def turn(d, q, part):
        first, size = part[:2]
        for k in range(kc):
            at = (q * kc + k) * V
            i_t[d, first:first + size, at:at + V] = i_all[d, q * kc + k, :, first:first + size].T

    def add(d, block, x, q, part):
        first, size, start = part
        piece = lax.dot_general(i_t[d, first:first + size, q * w:(q + 1) * w], x, (((1,), (0,)), ((), ())),
                                preferred_element_type=jnp.float32)
        to = pl.ds(start if isinstance(start, int) else pl.multiple_of(start, 128), size)
        if q == 0:
            acc[d, block, to] = piece
        else:
            acc[d, block, to] += piece

    own_row = lax.rem(lax.div(c, m) - r + R, R)
    own_at = pl.ds(pl.multiple_of(lax.rem(c, m) * V, V), V)

    def own_block(d, q, part):
        add(d, c, a_all[own_row, ks(q), own_at].reshape(w, N), q, part)

    for q in range(Q):
        own_a(q).wait()
        for d in range(1, R):
            row_a(R - d, q).wait_recv()
            col_start(d, q)
        own_i(q).wait()
        turn(0, q, whole)
        own_block(0, q, whole)

    for q in range(Q):
        for dc in order[::-1]:
            s = near(dc)
            here = az.at[s, ks(q)]
            remote(here, here, zsend.at[0, 0, q], zrecv.at[s, q], col=s).wait_recv()
            add(0, s, az[s, ks(q)].reshape(w, N), q, whole)

    def block(t, hi, bit):
        return (hi << (t + 1)) | (bit << t) | (l & ((1 << t) - 1))

    def halving(d, t, i, col):
        n = L >> (t + 1)
        hi = (l >> (t + 1)) ^ hi_order(n)[i]
        bit = (l >> t) & 1
        slot = n - 1 + hi
        give, keep = block(t, hi, 1 - bit), block(t, hi, bit)
        give, keep = (pl.ds(pl.multiple_of(b * rows, 8), rows) for b in (give, keep))
        if d == 0:
            cp = remote(acc.at[0, :, give], lay_buf.at[0, slot], osend.at[slot], orecv.at[slot], layer=l ^ (1 << t))
        else:
            cp = remote(acc.at[d, col, give], lay_buf.at[d, slot, col], lsend.at[d, slot, col], lrecv.at[d, slot, col],
                        layer=l ^ (1 << t))
        return cp, keep, slot

    def own_stage(t):
        for i in range(L >> (t + 1)):
            cp, keep, slot = halving(0, t, i, None)
            cp.wait_recv()
            acc[0, :, keep] += lay_buf[0, slot]
            if t + 1 < stages and i < L >> (t + 2):
                halving(0, t + 1, i, None)[0].start()

    for i in range(L >> 1):
        halving(0, 0, i, None)[0].start()

    c_order = [near(dc) for dc in order] + [c]
    mine = pl.ds(pl.multiple_of(l * rows, 8), rows)

    def first_stage_start(i):
        for d in range(1, R):
            for col in c_order:
                halving(d, 0, i, col)[0].start()

    def stage_end(t, i):
        for d in range(1, R):
            for col in c_order:
                cp, keep, slot = halving(d, t, i, col)
                cp.wait_recv()
                acc[d, col, keep] += lay_buf[d, slot, col]
                if t + 1 == stages:
                    row_sum(d, col).start()
                elif i < L >> (t + 2):
                    halving(d, t + 1, i, col)[0].start()

    for p, part in enumerate(parts):
        for q in range(Q):
            for d in range(1, R):
                row_i(R - d, q, p).wait_recv()
                turn(d, q, part)
                own_block(d, q, part)
                for dc in order:
                    s = near(dc)
                    add(d, s, az[s, ks(q)].reshape(w, N), q, part)
            if p == 0 and q == 0:
                own_stage(0)
            if p == 1 and q == min(1, Q - 1):
                stage_end(0, 0)
        if late:
            first_stage_start(p)

    def row_sum(d, col):
        return remote(acc.at[d, col, mine], row_buf.at[R - d, c], rsend.at[d, col], rrecv.at[R - d, c],
                      row=far_row(d), col=col)

    def col_sum(dc):
        return remote(acc.at[0, near(dc), mine], col_buf.at[c], csend.at[dc], crecv.at[c], col=near(dc))

    if not late:
        for i in range(L >> 1):
            first_stage_start(i)
    for t in range(1, stages):
        own_stage(t)
    for dc in order:
        col_sum(dc).start()
    for t in range(stages):
        for i in range(L >> (t + 1)):
            if not (late and t == 0 and i == 0):
                stage_end(t, i)
    total = acc[0, c, mine]
    for dc in order[::-1]:
        s = near(dc)
        remote(col_buf.at[s], col_buf.at[s], csend.at[dc], crecv.at[s], col=s).wait_recv()
        total += col_buf[s]
    for col in c_order[::-1]:
        for d in range(1, R):
            here = row_buf.at[d, col]
            remote(here, here, rsend.at[d, col], rrecv.at[d, col], row=far_row(d), col=col).wait_recv()
            total += row_buf[d, col]
    o_ref[...] = total

    for q in range(Q):
        for d in range(R):
            if d:
                row_a(d, q).wait_send()
                for p in range(len(parts)):
                    row_i(d, q, p).wait_send()
            for j in range(m):
                b, cp = col_a(d, j, q)

                @pl.when(b != c)
                def _():
                    cp.wait_send()
    for t in range(stages):
        for i in range(L >> (t + 1)):
            halving(0, t, i, None)[0].wait_send()
            for d in range(1, R):
                for col in c_order:
                    halving(d, t, i, col)[0].wait_send()
    for col in c_order:
        for d in range(1, R):
            row_sum(d, col).wait_send()
    for dc in order:
        col_sum(dc).wait_send()


def local(R, C, L, integrals, amplitudes, coulomb, row_gap, col_gap):
    K, V, M = integrals.shape
    V_row, N = amplitudes.shape[1:]
    rows = M // L
    Kr = K // R
    Q = Kr
    m = C // R
    slots = L - 1
    dma = pltpu.SemaphoreType.DMA
    vmem = pl.BlockSpec(memory_space=pltpu.VMEM)
    anyspace = pl.BlockSpec(memory_space=pl.ANY)
    own_rows = pl.pallas_call(
        functools.partial(kernel, R, C, L, Q),
        out_shape=jax.ShapeDtypeStruct((rows, N), jnp.float32),
        in_specs=[anyspace, anyspace],
        out_specs=vmem,
        scratch_shapes=[
            pltpu.VMEM((R, Kr, V_row, N), jnp.bfloat16),
            pltpu.VMEM((C, Kr, V, N), jnp.bfloat16),
            pltpu.VMEM((R, Kr, V, M), jnp.bfloat16),
            pltpu.VMEM((R, M, Kr * V), jnp.bfloat16),
            pltpu.VMEM((R, C, M, N), jnp.float32),
            pltpu.VMEM((R, slots, C, rows, N), jnp.float32),
            pltpu.VMEM((R, C, rows, N), jnp.float32),
            pltpu.VMEM((C, rows, N), jnp.float32),
            dma((R, Q)), dma((R, Q)),
            dma((2 * R, Q)), dma((2 * R, Q)),
            dma((R, m, Q)), dma((C, Q)),
            dma((slots,)), dma((slots,)),
            dma((R, slots, C)), dma((R, slots, C)),
            dma((R, C)), dma((R, C)),
            dma((C,)), dma((C,)),
        ],
        compiler_params=pltpu.CompilerParams(collective_id=0, has_side_effects=True),
    )(integrals, amplitudes)
    gap_sum = row_gap[:, None] + col_gap[None, :]
    return (coulomb.astype(jnp.float32) + own_rows) / gap_sum


def solution(mesh):
    R, C, L = (mesh.shape[a] for a in ("row", "col", "layer"))
    placed = (
        P("layer", "col", "row"),
        P("layer", "row", "col"),
        P(("row", "layer"), "col"),
        P(("row", "layer")),
        P("col"),
    )
    return jax.shard_map(
        functools.partial(local, R, C, L), mesh=mesh, in_specs=placed, out_specs=P(("row", "layer"), "col"),
        check_vma=False,
    )
```

profile of v0, /device:TPU:0, one launch (start us, length us, event | category | flops | bytes accessed | tf_op | source)
XLA Modules:
  0.0 78.4 jit_solution(14986146369940208762)
XLA Ops:
  0.0 0.0 copy-start.1
  0.0 0.0 copy-start.2
  0.0 0.0 copy-start
  0.0 76.9 %shard_map.55 = f32[96,128]{1,0:T(8,128)} custom-call(bf16[16,256,384]{2,1,0:T(8,128)(2,1)} %i_ref.1, bf16[16,512,128]{2,1,0:T(8,128)(2,1)} %a_ref.1), custom_call_target="tpu_custom_call" | custom-call | tf_op jit(solution)/shard_map/pallas_call | solution.py:279
  76.9 0.0 copy-done.1
  76.9 0.0 copy-done.2
  76.9 0.0 copy-done
  76.9 1.5 %add_divide_fusion = f32[96,128]{1,0:T(8,128)} fusion(f32[96,128]{1,0:T(8,128)} %shard_map.55, bf16[96,128]{1,0:T(8,128)(2,1)S(1)} %copy-done, f32[128]{0:T(128)S(1)} %copy-done.1, f32[96]{0:T(128)S(1)} %copy-done.2), kind=kLoop, calls=%fused_computation | loop fusion | flops 49152 | bytes 123776 | tf_op jit(solution)/shard_map/div | solution.py:304
Async XLA Ops:
  0.0 76.9 %copy-start.1 = (f32[128]{0:T(128)S(1)}, f32[128]{0:T(128)}, u32[]{:S(2)}) copy-start(f32[128]{0:T(128)} %param.9) | copy-start | bytes 1540
  0.0 76.9 %copy-start.2 = (f32[96]{0:T(128)S(1)}, f32[96]{0:T(128)}, u32[]{:S(2)}) copy-start(f32[96]{0:T(128)} %param.8) | copy-start | bytes 1156
  0.0 76.9 %copy-start = (bf16[96,128]{1,0:T(8,128)(2,1)S(1)}, bf16[96,128]{1,0:T(8,128)(2,1)}, u32[]{:S(2)}) copy-start(bf16[96,128]{1,0:T(8,128)(2,1)} %param.7) | copy-start | bytes 73732
where the time goes:
time: 78.6 us; the launch traced here: 78.4 us
  Pallas kernels  76.9 us (98%)
  other arithmetic  1.51 us (2%)
    pallas_call x1, Pallas kernels, local(): pl.pallas_call(functools.partial(kernel, R, C, L, Q), out_shape=jax.Shape...  76.9 us

commit v1 on v0

--- a/solution.py
+++ b/solution.py
@@ -265,7 +265,7 @@
         col_sum(dc).wait_send()
 
 
-def local(R, C, L, integrals, amplitudes, coulomb, row_gap, col_gap):
+def general_call(R, C, L, integrals, amplitudes):
     K, V, M = integrals.shape
     V_row, N = amplitudes.shape[1:]
     rows = M // L
@@ -276,7 +276,7 @@
     dma = pltpu.SemaphoreType.DMA
     vmem = pl.BlockSpec(memory_space=pltpu.VMEM)
     anyspace = pl.BlockSpec(memory_space=pl.ANY)
-    own_rows = pl.pallas_call(
+    return pl.pallas_call(
         functools.partial(kernel, R, C, L, Q),
         out_shape=jax.ShapeDtypeStruct((rows, N), jnp.float32),
         in_specs=[anyspace, anyspace],
@@ -300,6 +300,387 @@
         ],
         compiler_params=pltpu.CompilerParams(collective_id=0, has_side_effects=True),
     )(integrals, amplitudes)
+
+
+def swift(R, C, L, T, i_ref, a_ref, o_ref,
+          a_x, az, i_in, i_s, i_t, acc, last, core_buf, x_buf, z_buf, y_out, y_buf, last_buf,
+          own, iown, asend, arecv, isend, irecv, zsend, zrecv,
+          csend, crecv, xsend, xrecv, wsend, wrecv, ysend, yrecv, lsend, lrecv, there):
+    r, c, l = lax.axis_index("row"), lax.axis_index("col"), lax.axis_index("layer")
+    K, V, M = i_ref.shape
+    N = a_ref.shape[2]
+    Kr = K // R
+    W = Kr * V
+    m = C // R
+    rows = M // L
+    half_rows = 2 * rows
+    body = rows - T
+    o = 1 - r
+    x, core = lax.div(l, 2), lax.rem(l, 2)
+    home = lax.div(c, m) == r
+
+    def remote(src, dst, ss, rs, **to):
+        where = {"row": r, "col": c, "layer": l}
+        where.update(to)
+        return pltpu.make_async_remote_copy(src_ref=src, dst_ref=dst, send_sem=ss, recv_sem=rs,
+                                            device_id=where, device_id_type=MESH)
+
+    def signal(sem, **to):
+        where = {"row": r, "col": c, "layer": l}
+        where.update(to)
+        pl.semaphore_signal(sem, inc=1, device_id=where, device_id_type=MESH)
+
+    def at(start, size, unit):
+        return pl.ds(pl.multiple_of(start, unit), size)
+
+    sib, opp = l ^ 1, l ^ 2
+
+    def local_a(q):
+        return pltpu.make_async_copy(a_ref.at[r * Kr + q, at(lax.rem(c, m) * V, V, V)], az.at[c, q], own.at[q])
+
+    def cross_a(q):
+        return pltpu.make_async_copy(a_x.at[q, at(lax.rem(c, m) * V, V, V)], az.at[c, q], own.at[q])
+
+    def local_i(k):
+        return pltpu.make_async_copy(i_ref.at[k], i_in.at[k], iown.at[k])
+
+    barrier = pltpu.get_barrier_semaphore()
+    signal(barrier, row=o)
+    signal(barrier, layer=sib)
+    signal(barrier, layer=opp)
+
+    @pl.when(c > 0)
+    def _():
+        signal(barrier, col=c - 1)
+
+    @pl.when(c < C - 1)
+    def _():
+        signal(barrier, col=c + 1)
+
+    for k in range(Kr):
+        local_i(o * Kr + k).start()
+    for k in range(Kr):
+        local_i(r * Kr + k).start()
+
+    @pl.when(home)
+    def _():
+        for q in range(Kr):
+            local_a(q).start()
+
+    pl.semaphore_wait(barrier, 3 + (c > 0).astype(jnp.int32) + (c < C - 1).astype(jnp.int32))
+
+    def row_a(q):
+        return remote(a_ref.at[o * Kr + q], a_x.at[q], asend.at[q], arecv.at[q], row=o)
+
+    for q in range(Kr):
+        row_a(q).start()
+
+    for t in range(2, C):
+        @pl.when((c >= 1) & (c + t - 1 < C))
+        def _():
+            signal(there.at[0, t], col=c - 1)
+
+        @pl.when((c + 1 < C) & (c - t + 1 >= 0))
+        def _():
+            signal(there.at[1, t], col=c + 1)
+
+        @pl.when(c + t < C)
+        def _():
+            pl.semaphore_wait(there.at[0, t], 1)
+
+        @pl.when(c - t >= 0)
+        def _():
+            pl.semaphore_wait(there.at[1, t], 1)
+
+    def col_a(d, j, q):
+        b = (o if d else r) * m + j
+        span = pl.ds(j * V, V)
+        src = a_x.at[q, span] if d else a_ref.at[r * Kr + q, span]
+        return b, remote(src, az.at[c, q], zsend.at[d, j, q], zrecv.at[c, q], col=b)
+
+    def col_start(d, q):
+        for j in range(m):
+            b, cp = col_a(d, j, q)
+
+            @pl.when(b != c)
+            def _():
+                cp.start()
+
+    ahead = 2
+    for q in range(ahead):
+        col_start(0, q)
+
+    def turn(dst, k, kk):
+        dst[:, kk * V:(kk + 1) * V] = i_in[k].T
+
+    other = (1 - x) * half_rows
+    mine = x * half_rows
+    groups = [(other, rows), (other + rows, rows), (mine, body), (mine + rows, body),
+              (mine + body, T), (mine + rows + body, T)]
+
+    def row_i(g):
+        start, size = groups[g]
+        span = at(start, size, 16)
+        return remote(i_s.at[span], i_t.at[1, span], isend.at[g], irecv.at[g], row=o)
+
+    per = 2 * Kr // Kr
+    for q in range(Kr):
+        row_a(q).wait_recv()
+        col_start(1, q)
+
+        @pl.when(jnp.logical_not(home))
+        def _():
+            cross_a(q).start()
+
+        if q + ahead < Kr:
+            col_start(0, q + ahead)
+        for kk in range(per * q, per * q + per):
+            if kk < Kr:
+                local_i(o * Kr + kk).wait()
+                turn(i_s, o * Kr + kk, kk)
+                if kk == Kr - 1:
+                    for g in range(len(groups)):
+                        row_i(g).start()
+            else:
+                local_i(r * Kr + kk - Kr).wait()
+                turn(i_t.at[0], r * Kr + kk - Kr, kk - Kr)
+
+    near, far = lax.div(c, m) * m, (1 - lax.div(c, m)) * m
+    first = [near, far]
+
+    def wait_piece(s):
+        for q in range(Kr):
+            @pl.when(s == c)
+            def _():
+                local_a(q).wait()
+
+            @pl.when(s != c)
+            def _():
+                here = az.at[s, q]
+                remote(here, here, zsend.at[0, 0, q], zrecv.at[s, q], col=s).wait_recv()
+
+    def wide(h):
+        return jnp.concatenate([az[first[h] + j].reshape(W, N) for j in range(m)], axis=1)
+
+    def product(d, start, size, right):
+        return lax.dot_general(i_t[d, at(start, size, 16)], right, (((1,), (0,)), ((), ())),
+                               preferred_element_type=jnp.float32)
+
+    def fill(d, h, start, size, right):
+        piece = product(d, start, size, right)
+        for j in range(m):
+            acc[d, first[h] + j, at(start, size, 16)] = piece[:, j * N:(j + 1) * N]
+
+    def pair(h):
+        return pl.ds(first[h], m)
+
+    def block(b, size=rows):
+        return at(b * rows, size, 16)
+
+    def core_copy(d, h, keep):
+        xx = x if keep else 1 - x
+        size = body if d and keep else rows
+        give = block(2 * xx + 1 - core, size)
+        return remote(acc.at[d, pair(h), give], core_buf.at[d, h, keep, :, pl.ds(0, size)],
+                      csend.at[d, h, keep], crecv.at[d, h, keep], layer=sib)
+
+    def core_end(d, h, keep):
+        xx = x if keep else 1 - x
+        size = body if d and keep else rows
+        core_copy(d, h, keep).wait_recv()
+        acc[d, pair(h), block(2 * xx + core, size)] += core_buf[d, h, keep, :, :size]
+
+    def x_copy(d, h):
+        return remote(acc.at[d, pair(h), block(2 * (1 - x) + core)], x_buf.at[d, h], xsend.at[d, h], xrecv.at[d, h], layer=opp)
+
+    def x_end(d, h):
+        x_copy(d, h).wait_recv()
+        if d:
+            acc[d, pair(h), block(l, body)] += x_buf[d, h, :, :body]
+            acc[d, pair(h), at(l * rows + body, T, 16)] = x_buf[d, h, :, body:]
+        else:
+            acc[d, pair(h), block(l)] += x_buf[d, h]
+
+    def z_copy(d, h, j):
+        s = first[h] + j
+        return s, remote(acc.at[d, s, block(l)], z_buf.at[d, c], wsend.at[d, h, j], wrecv.at[d, c], col=s)
+
+    def z_start(d, h):
+        for j in range(m):
+            s, cp = z_copy(d, h, j)
+
+            @pl.when(s != c)
+            def _():
+                cp.start()
+
+    def z_end(d):
+        total = acc[d, c, block(l)]
+        for dc in range(1, C):
+            s = lax.rem(c + dc, C)
+            here = z_buf.at[d, s]
+            remote(here, here, wsend.at[d, 0, 0], wrecv.at[d, s], col=s).wait_recv()
+            total += z_buf[d, s]
+        return total
+
+    for j in range(m):
+        wait_piece(near + j)
+    right = wide(0)
+    fill(0, 0, 0, M, right)
+    core_copy(0, 0, 0).start()
+    core_copy(0, 0, 1).start()
+    core_end(0, 0, 0)
+    x_copy(0, 0).start()
+    core_end(0, 0, 1)
+
+    for g in range(2):
+        row_i(g).wait_recv()
+    fill(1, 0, other, half_rows, right)
+    core_copy(1, 0, 0).start()
+    x_end(0, 0)
+    z_start(0, 0)
+    core_end(1, 0, 0)
+    x_copy(1, 0).start()
+
+    for j in range(m):
+        wait_piece(far + j)
+    right = wide(1)
+    fill(0, 1, 0, M, right)
+    core_copy(0, 1, 0).start()
+    core_copy(0, 1, 1).start()
+    fill(1, 1, other, half_rows, right)
+    core_copy(1, 1, 0).start()
+    core_end(0, 1, 0)
+    x_copy(0, 1).start()
+    core_end(1, 1, 0)
+    x_copy(1, 1).start()
+    core_end(0, 1, 1)
+
+    for g in range(2, 4):
+        row_i(g).wait_recv()
+    for h in range(2):
+        right = wide(h)
+        for i in range(2):
+            fill(1, h, mine + i * rows, body, right)
+        core_copy(1, h, 1).start()
+    x_end(0, 1)
+    z_start(0, 1)
+    for h in range(2):
+        core_end(1, h, 1)
+
+    def last_copy(i, s):
+        return remote(last.at[i, s], last_buf.at[core, c], lsend.at[i, s], lrecv.at[core, c],
+                      row=o, col=s, layer=2 * x + i)
+
+    for g in range(4, 6):
+        row_i(g).wait_recv()
+    for h in range(2):
+        right = wide(h)
+        for i in range(2):
+            piece = product(1, mine + i * rows + body, T, right)
+            for j in range(m):
+                last[i, first[h] + j] = piece[:, j * N:(j + 1) * N]
+    for dc in range(C):
+        for i in range(2):
+            last_copy(i, c ^ (C - 1 - dc)).start()
+
+    for h in range(2):
+        x_end(1, h)
+        z_start(1, h)
+    total = z_end(0)
+    y_out[...] = z_end(1)
+
+    def y_copy():
+        return remote(y_out, y_buf, ysend, yrecv, row=o)
+
+    y_copy().start()
+    tail = jnp.zeros((T, N), jnp.float32)
+    for i in range(2):
+        for dc in range(C):
+            s = c ^ dc
+            here = last_buf.at[i, s]
+            remote(here, here, lsend.at[0, 0], lrecv.at[i, s], row=o, col=s, layer=2 * x + i).wait_recv()
+            tail += last_buf[i, s]
+    y_copy().wait_recv()
+    total += y_buf[...]
+    o_ref[:body] = total[:body]
+    o_ref[body:] = total[body:] + tail
+
+    for q in range(Kr):
+        row_a(q).wait_send()
+        for d in range(2):
+            for j in range(m):
+                b, cp = col_a(d, j, q)
+
+                @pl.when(b != c)
+                def _():
+                    cp.wait_send()
+    for g in range(len(groups)):
+        row_i(g).wait_send()
+    for d in range(2):
+        for h in range(2):
+            for keep in range(2):
+                core_copy(d, h, keep).wait_send()
+            x_copy(d, h).wait_send()
+            for j in range(m):
+                s, cp = z_copy(d, h, j)
+
+                @pl.when(s != c)
+                def _():
+                    cp.wait_send()
+    for s in range(C):
+        for i in range(2):
+            last_copy(i, s).wait_send()
+    y_copy().wait_send()
+
+
+def swift_call(R, C, L, integrals, amplitudes):
+    K, V, M = integrals.shape
+    V_row, N = amplitudes.shape[1:]
+    rows = M // L
+    Kr = K // R
+    m = C // R
+    T = 16
+    dma = pltpu.SemaphoreType.DMA
+    f32, bf16 = jnp.float32, jnp.bfloat16
+    anyspace = pl.BlockSpec(memory_space=pl.ANY)
+    return pl.pallas_call(
+        functools.partial(swift, R, C, L, T),
+        out_shape=jax.ShapeDtypeStruct((rows, N), f32),
+        in_specs=[anyspace, anyspace],
+        out_specs=pl.BlockSpec(memory_space=pltpu.VMEM),
+        scratch_shapes=[
+            pltpu.VMEM((Kr, V_row, N), bf16),
+            pltpu.VMEM((C, Kr, V, N), bf16),
+            pltpu.VMEM((K, V, M), bf16),
+            pltpu.VMEM((M, Kr * V), bf16),
+            pltpu.VMEM((2, M, Kr * V), bf16),
+            pltpu.VMEM((2, C, M, N), f32),
+            pltpu.VMEM((2, C, T, N), f32),
+            pltpu.VMEM((2, 2, 2, m, rows, N), f32),
+            pltpu.VMEM((2, 2, m, rows, N), f32),
+            pltpu.VMEM((2, C, rows, N), f32),
+            pltpu.VMEM((rows, N), f32),
+            pltpu.VMEM((rows, N), f32),
+            pltpu.VMEM((2, C, T, N), f32),
+            dma((Kr,)), dma((K,)),
+            dma((Kr,)), dma((Kr,)),
+            dma((6,)), dma((6,)),
+            dma((2, m, Kr)), dma((C, Kr)),
+            dma((2, 2, 2)), dma((2, 2, 2)),
+            dma((2, 2)), dma((2, 2)),
+            dma((2, 2, m)), dma((2, C)),
+            dma, dma,
+            dma((2, C)), dma((2, C)),
+            pltpu.SemaphoreType.REGULAR((2, C)),
+        ],
+        compiler_params=pltpu.CompilerParams(collective_id=0, has_side_effects=True),
+    )(integrals, amplitudes)
+
+
+def local(R, C, L, integrals, amplitudes, coulomb, row_gap, col_gap):
+    swift_fits = R == 2 and C == 4 and L == 4 and integrals.shape[2] % (16 * L) == 0
+    call = swift_call if swift_fits else general_call
+    own_rows = call(R, C, L, integrals, amplitudes)
     gap_sum = row_gap[:, None] + col_gap[None, :]
     return (coulomb.astype(jnp.float32) + own_rows) / gap_sum
 

time: 78.6 us -> 78.5 us (level)
  no operation moved by 1% of the time
where the time goes in v1:
time: 78.5 us; the launch traced here: 78.3 us
  Pallas kernels  76.7 us (98%)
  other arithmetic  1.51 us (2%)
    pallas_call x1, Pallas kernels, swift_call(): pl.pallas_call(functools.partial(swift, R, C, L, T), out_shape=jax.ShapeD...  76.7 us

profile of v1, /device:TPU:0, one launch (start us, length us, event | category | flops | bytes accessed | tf_op | source)
XLA Modules:
  0.0 78.3 jit_solution(4149802148361492727)
XLA Ops:
  0.0 0.0 copy-start.1
  0.0 0.0 copy-start.2
  0.0 0.0 copy-start
  0.0 76.7 %shard_map.55 = f32[96,128]{1,0:T(8,128)} custom-call(bf16[16,256,384]{2,1,0:T(8,128)(2,1)} %i_ref.1, bf16[16,512,128]{2,1,0:T(8,128)(2,1)} %a_ref.1), custom_call_target="tpu_custom_call" | custom-call | tf_op jit(solution)/shard_map/pallas_call | solution.py:646
  76.8 0.0 copy-done.1
  76.8 0.0 copy-done.2
  76.8 0.0 copy-done
  76.8 1.5 %add_divide_fusion = f32[96,128]{1,0:T(8,128)} fusion(f32[96,128]{1,0:T(8,128)} %shard_map.55, bf16[96,128]{1,0:T(8,128)(2,1)S(1)} %copy-done, f32[128]{0:T(128)S(1)} %copy-done.1, f32[96]{0:T(128)S(1)} %copy-done.2), kind=kLoop, calls=%fused_computation | loop fusion | flops 49152 | bytes 123776 | tf_op jit(solution)/shard_map/div | solution.py:685
Async XLA Ops:
  0.0 76.8 %copy-start.1 = (f32[128]{0:T(128)S(1)}, f32[128]{0:T(128)}, u32[]{:S(2)}) copy-start(f32[128]{0:T(128)} %param.9) | copy-start | bytes 1540
  0.0 76.8 %copy-start.2 = (f32[96]{0:T(128)S(1)}, f32[96]{0:T(128)}, u32[]{:S(2)}) copy-start(f32[96]{0:T(128)} %param.8) | copy-start | bytes 1156
  0.0 76.8 %copy-start = (bf16[96,128]{1,0:T(8,128)(2,1)S(1)}, bf16[96,128]{1,0:T(8,128)(2,1)}, u32[]{:S(2)}) copy-start(bf16[96,128]{1,0:T(8,128)(2,1)} %param.7) | copy-start | bytes 73732

commit v2 on v1

--- a/solution.py
+++ b/solution.py
@@ -303,9 +303,9 @@
 
 
 def swift(R, C, L, T, i_ref, a_ref, o_ref,
-          a_x, az, i_in, i_s, i_t, acc, last, core_buf, x_buf, z_buf, y_out, y_buf, last_buf,
+          a_x, az, i_in, i_s, i_t, acc, last, core_buf, x_buf, z_buf, y_out, y_buf, last_buf, hi_buf, lo_buf,
           own, iown, asend, arecv, isend, irecv, zsend, zrecv,
-          csend, crecv, xsend, xrecv, wsend, wrecv, ysend, yrecv, lsend, lrecv, there):
+          csend, crecv, xsend, xrecv, wsend, wrecv, ysend, yrecv, lsend, lrecv, hsend, hrecv, there):
     r, c, l = lax.axis_index("row"), lax.axis_index("col"), lax.axis_index("layer")
     K, V, M = i_ref.shape
     N = a_ref.shape[2]
@@ -315,9 +315,13 @@
     rows = M // L
     half_rows = 2 * rows
     body = rows - T
+    low = rows // 2 // 16 * 16
     o = 1 - r
     x, core = lax.div(l, 2), lax.rem(l, 2)
     home = lax.div(c, m) == r
+    away = jnp.logical_not(home)
+    outer = (c == 0) | (c == C - 1)
+    inner = jnp.logical_not(outer)
 
     def remote(src, dst, ss, rs, **to):
         where = {"row": r, "col": c, "layer": l}
@@ -357,40 +361,15 @@
     def _():
         signal(barrier, col=c + 1)
 
-    for k in range(Kr):
-        local_i(o * Kr + k).start()
-    for k in range(Kr):
-        local_i(r * Kr + k).start()
-
-    @pl.when(home)
-    def _():
-        for q in range(Kr):
-            local_a(q).start()
-
     pl.semaphore_wait(barrier, 3 + (c > 0).astype(jnp.int32) + (c < C - 1).astype(jnp.int32))
 
-    def row_a(q):
-        return remote(a_ref.at[o * Kr + q], a_x.at[q], asend.at[q], arecv.at[q], row=o)
+    def row_a(q, j):
+        span = pl.ds(j * V, V)
+        return remote(a_ref.at[o * Kr + q, span], a_x.at[q, span], asend.at[q, j], arecv.at[q, j], row=o)
 
     for q in range(Kr):
-        row_a(q).start()
-
-    for t in range(2, C):
-        @pl.when((c >= 1) & (c + t - 1 < C))
-        def _():
-            signal(there.at[0, t], col=c - 1)
-
-        @pl.when((c + 1 < C) & (c - t + 1 >= 0))
-        def _():
-            signal(there.at[1, t], col=c + 1)
-
-        @pl.when(c + t < C)
-        def _():
-            pl.semaphore_wait(there.at[0, t], 1)
-
-        @pl.when(c - t >= 0)
-        def _():
-            pl.semaphore_wait(there.at[1, t], 1)
+        for j in range(m):
+            row_a(q, j).start()
 
     def col_a(d, j, q):
         b = (o if d else r) * m + j
@@ -398,25 +377,63 @@
         src = a_x.at[q, span] if d else a_ref.at[r * Kr + q, span]
         return b, remote(src, az.at[c, q], zsend.at[d, j, q], zrecv.at[c, q], col=b)
 
-    def col_start(d, q):
-        for j in range(m):
-            b, cp = col_a(d, j, q)
-
-            @pl.when(b != c)
-            def _():
-                cp.start()
-
-    ahead = 2
-    for q in range(ahead):
-        col_start(0, q)
+    def col_start(d, *qs, js=range(m)):
+        for q in qs:
+            for j in js:
+                b, cp = col_a(d, j, q)
+
+                @pl.when(b != c)
+                def _():
+                    cp.start()
+
+    ahead, turnover = 3, Kr - 2
+
+    @pl.when(home)
+    def _():
+        col_start(0, *range(ahead))
+
+    @pl.when(home & inner)
+    def _():
+        col_start(0, *range(ahead, Kr))
+
+    for t in range(2, C):
+        @pl.when((c >= 1) & (c + t - 1 < C))
+        def _():
+            signal(there.at[0, t], col=c - 1)
+
+        @pl.when((c + 1 < C) & (c - t + 1 >= 0))
+        def _():
+            signal(there.at[1, t], col=c + 1)
+
+        @pl.when(c + t < C)
+        def _():
+            pl.semaphore_wait(there.at[0, t], 1)
+
+        @pl.when(c - t >= 0)
+        def _():
+            pl.semaphore_wait(there.at[1, t], 1)
+
+    @pl.when(away & outer)
+    def _():
+        col_start(0, *range(Kr))
+
+    for k in range(Kr):
+        local_i(o * Kr + k).start()
+    for k in range(Kr):
+        local_i(r * Kr + k).start()
+
+    @pl.when(home)
+    def _():
+        for q in range(Kr):
+            local_a(q).start()
 
     def turn(dst, k, kk):
         dst[:, kk * V:(kk + 1) * V] = i_in[k].T
 
     other = (1 - x) * half_rows
     mine = x * half_rows
-    groups = [(other, rows), (other + rows, rows), (mine, body), (mine + rows, body),
-              (mine + body, T), (mine + rows + body, T)]
+    groups = [(other, rows), (other + rows, rows), (mine, low), (mine + rows, low),
+              (mine + low, body - low), (mine + rows + low, body - low), (mine + body, T), (mine + rows + body, T)]
 
     def row_i(g):
         start, size = groups[g]
@@ -425,15 +442,32 @@
 
     per = 2 * Kr // Kr
     for q in range(Kr):
-        row_a(q).wait_recv()
-        col_start(1, q)
-
-        @pl.when(jnp.logical_not(home))
+        for j in range(m):
+            row_a(q, j).wait_recv()
+            if q < turnover:
+                @pl.when(outer | away)
+                def _():
+                    col_start(1, q, js=[j])
+            else:
+                col_start(1, q, js=[j])
+
+        @pl.when(away)
         def _():
             cross_a(q).start()
 
-        if q + ahead < Kr:
-            col_start(0, q + ahead)
+        if q == turnover:
+            @pl.when(inner & home)
+            def _():
+                col_start(1, *range(turnover))
+
+            @pl.when(inner & away)
+            def _():
+                col_start(0, *range(Kr))
+
+            @pl.when(outer & home)
+            def _():
+                col_start(0, *range(ahead, Kr))
+
         for kk in range(per * q, per * q + per):
             if kk < Kr:
                 local_i(o * Kr + kk).wait()
@@ -445,8 +479,8 @@
                 local_i(r * Kr + kk - Kr).wait()
                 turn(i_t.at[0], r * Kr + kk - Kr, kk - Kr)
 
-    near, far = lax.div(c, m) * m, (1 - lax.div(c, m)) * m
-    first = [near, far]
+    side = lax.div(c, m)
+    units = [(side * m, m), ((1 - side) * (C - 1), 1), (1 + (1 - side), 1)]
 
     def wait_piece(s):
         for q in range(Kr):
@@ -459,154 +493,198 @@
                 here = az.at[s, q]
                 remote(here, here, zsend.at[0, 0, q], zrecv.at[s, q], col=s).wait_recv()
 
-    def wide(h):
-        return jnp.concatenate([az[first[h] + j].reshape(W, N) for j in range(m)], axis=1)
+    def columns(us):
+        return [units[u][0] + j for u in us for j in range(units[u][1])]
+
+    def wide(us):
+        return jnp.concatenate([az[s].reshape(W, N) for s in columns(us)], axis=1)
 
     def product(d, start, size, right):
         return lax.dot_general(i_t[d, at(start, size, 16)], right, (((1,), (0,)), ((), ())),
                                preferred_element_type=jnp.float32)
 
-    def fill(d, h, start, size, right):
+    def fill(d, us, start, size, right):
         piece = product(d, start, size, right)
-        for j in range(m):
-            acc[d, first[h] + j, at(start, size, 16)] = piece[:, j * N:(j + 1) * N]
-
-    def pair(h):
-        return pl.ds(first[h], m)
+        for j, s in enumerate(columns(us)):
+            acc[d, s, at(start, size, 16)] = piece[:, j * N:(j + 1) * N]
+
+    def pair(u):
+        return pl.ds(*units[u])
 
     def block(b, size=rows):
         return at(b * rows, size, 16)
 
-    def core_copy(d, h, keep):
-        xx = x if keep else 1 - x
-        size = body if d and keep else rows
-        give = block(2 * xx + 1 - core, size)
-        return remote(acc.at[d, pair(h), give], core_buf.at[d, h, keep, :, pl.ds(0, size)],
-                      csend.at[d, h, keep], crecv.at[d, h, keep], layer=sib)
-
-    def core_end(d, h, keep):
-        xx = x if keep else 1 - x
-        size = body if d and keep else rows
-        core_copy(d, h, keep).wait_recv()
-        acc[d, pair(h), block(2 * xx + core, size)] += core_buf[d, h, keep, :, :size]
-
-    def x_copy(d, h):
-        return remote(acc.at[d, pair(h), block(2 * (1 - x) + core)], x_buf.at[d, h], xsend.at[d, h], xrecv.at[d, h], layer=opp)
-
-    def x_end(d, h):
-        x_copy(d, h).wait_recv()
-        if d:
-            acc[d, pair(h), block(l, body)] += x_buf[d, h, :, :body]
-            acc[d, pair(h), at(l * rows + body, T, 16)] = x_buf[d, h, :, body:]
-        else:
-            acc[d, pair(h), block(l)] += x_buf[d, h]
-
-    def z_copy(d, h, j):
-        s = first[h] + j
-        return s, remote(acc.at[d, s, block(l)], z_buf.at[d, c], wsend.at[d, h, j], wrecv.at[d, c], col=s)
-
-    def z_start(d, h):
-        for j in range(m):
-            s, cp = z_copy(d, h, j)
+    def core_span(d, keep):
+        if d and keep:
+            return (0, low) if keep == 1 else (low, body - low)
+        return (0, rows)
+
+    def core_copy(d, u, keep):
+        start, size = core_span(d, keep)
+        give = 2 * (x if keep else 1 - x) + 1 - core
+        return remote(acc.at[d, pair(u), at(give * rows + start, size, 16)],
+                      core_buf.at[d, u, min(keep, 1), pl.ds(0, units[u][1]), pl.ds(start, size)],
+                      csend.at[d, u, keep], crecv.at[d, u, keep], layer=sib)
+
+    def core_end(d, u, keep):
+        start, size = core_span(d, keep)
+        have = 2 * (x if keep else 1 - x) + core
+        core_copy(d, u, keep).wait_recv()
+        acc[d, pair(u), at(have * rows + start, size, 16)] += core_buf[d, u, min(keep, 1), :units[u][1], start:start + size]
+
+    def x_copy(d, u):
+        return remote(acc.at[d, pair(u), block(2 * (1 - x) + core)], x_buf.at[d, u, pl.ds(0, units[u][1])],
+                      xsend.at[d, u], xrecv.at[d, u], layer=opp)
+
+    def x_add(d, u, start, size):
+        acc[d, pair(u), at(l * rows + start, size, 16)] += x_buf[d, u, :units[u][1], start:start + size]
+
+    def z_size(d):
+        return low if d else rows
+
+    def z_copy(d, u, j):
+        s = units[u][0] + j
+        return s, remote(acc.at[d, s, block(l, z_size(d))], z_buf.at[d, c, pl.ds(0, z_size(d))],
+                         wsend.at[d, u, j], wrecv.at[d, c], col=s)
+
+    def z_start(d, u):
+        for j in range(units[u][1]):
+            s, cp = z_copy(d, u, j)
 
             @pl.when(s != c)
             def _():
                 cp.start()
 
-    def z_end(d):
-        total = acc[d, c, block(l)]
-        for dc in range(1, C):
-            s = lax.rem(c + dc, C)
-            here = z_buf.at[d, s]
-            remote(here, here, wsend.at[d, 0, 0], wrecv.at[d, s], col=s).wait_recv()
-            total += z_buf[d, s]
-        return total
-
-    for j in range(m):
-        wait_piece(near + j)
-    right = wide(0)
-    fill(0, 0, 0, M, right)
-    core_copy(0, 0, 0).start()
-    core_copy(0, 0, 1).start()
-    core_end(0, 0, 0)
-    x_copy(0, 0).start()
-    core_end(0, 0, 1)
+    def z_wait(d, s):
+        here = z_buf.at[d, s, pl.ds(0, z_size(d))]
+        remote(here, here, wsend.at[d, 0, 0], wrecv.at[d, s], col=s).wait_recv()
+
+    def hi_copy(s):
+        return remote(acc.at[1, s, at(l * rows + low, rows - low, 16)], hi_buf.at[c], hsend.at[0, s], hrecv.at[0, c], row=o, col=s)
+
+    def lo_copy():
+        s = units[2][0]
+        return remote(acc.at[1, s, block(l, low)], lo_buf.at[lax.rem(c, m)], hsend.at[1, 0], hrecv.at[1, lax.rem(c, m)], row=o, col=s)
+
+    for s in columns([0, 1]):
+        wait_piece(s)
+    for u in (0, 1):
+        fill(0, [u], 0, M, wide([u]))
+        core_copy(0, u, 0).start()
+        core_copy(0, u, 1).start()
+    for u in (0, 1):
+        core_end(0, u, 0)
+        x_copy(0, u).start()
+    for u in (0, 1):
+        core_end(0, u, 1)
 
     for g in range(2):
         row_i(g).wait_recv()
-    fill(1, 0, other, half_rows, right)
-    core_copy(1, 0, 0).start()
-    x_end(0, 0)
-    z_start(0, 0)
-    core_end(1, 0, 0)
-    x_copy(1, 0).start()
-
-    for j in range(m):
-        wait_piece(far + j)
-    right = wide(1)
-    fill(0, 1, 0, M, right)
-    core_copy(0, 1, 0).start()
-    core_copy(0, 1, 1).start()
-    fill(1, 1, other, half_rows, right)
-    core_copy(1, 1, 0).start()
-    core_end(0, 1, 0)
-    x_copy(0, 1).start()
-    core_end(1, 1, 0)
-    x_copy(1, 1).start()
-    core_end(0, 1, 1)
+    for u in (0, 1):
+        fill(1, [u], other, half_rows, wide([u]))
+        core_copy(1, u, 0).start()
+    for u in (0, 1):
+        x_copy(0, u).wait_recv()
+        x_add(0, u, 0, rows)
+        z_start(0, u)
+    for u in (0, 1):
+        core_end(1, u, 0)
+        x_copy(1, u).start()
 
     for g in range(2, 4):
         row_i(g).wait_recv()
-    for h in range(2):
-        right = wide(h)
+    for u in (0, 1):
+        right = wide([u])
         for i in range(2):
-            fill(1, h, mine + i * rows, body, right)
-        core_copy(1, h, 1).start()
-    x_end(0, 1)
-    z_start(0, 1)
-    for h in range(2):
-        core_end(1, h, 1)
+            fill(1, [u], mine + i * rows, low, right)
+        core_copy(1, u, 1).start()
+    for u in (0, 1):
+        core_end(1, u, 1)
+        x_copy(1, u).wait_recv()
+        x_add(1, u, 0, low)
+        z_start(1, u)
+
+    for s in columns([2]):
+        wait_piece(s)
+    right = wide([2])
+    fill(0, [2], 0, M, right)
+    core_copy(0, 2, 0).start()
+    core_copy(0, 2, 1).start()
+    fill(1, [2], other, half_rows, right)
+    core_copy(1, 2, 0).start()
+    core_end(0, 2, 0)
+    x_copy(0, 2).start()
+    for i in range(2):
+        fill(1, [2], mine + i * rows, low, right)
+    core_copy(1, 2, 1).start()
+    core_end(1, 2, 0)
+    x_copy(1, 2).start()
+    core_end(0, 2, 1)
+    core_end(1, 2, 1)
+
+    for g in range(4, 6):
+        row_i(g).wait_recv()
+    for us in ([0], [1, 2]):
+        right = wide(us)
+        for i in range(2):
+            fill(1, us, mine + i * rows + low, body - low, right)
+        for u in us:
+            core_copy(1, u, 2).start()
+    x_copy(0, 2).wait_recv()
+    x_add(0, 2, 0, rows)
+    z_start(0, 2)
+
+    def high_start(u):
+        x_add(1, u, low, body - low)
+        acc[1, pair(u), at(l * rows + body, T, 16)] = x_buf[1, u, :units[u][1], body:]
+        for s in columns([u]):
+            hi_copy(s).start()
+
+    for u in (0, 1):
+        core_end(1, u, 2)
+        high_start(u)
 
     def last_copy(i, s):
         return remote(last.at[i, s], last_buf.at[core, c], lsend.at[i, s], lrecv.at[core, c],
                       row=o, col=s, layer=2 * x + i)
 
-    for g in range(4, 6):
+    for g in range(6, 8):
         row_i(g).wait_recv()
-    for h in range(2):
-        right = wide(h)
+    for us in ([0], [1, 2]):
+        right = wide(us)
         for i in range(2):
             piece = product(1, mine + i * rows + body, T, right)
-            for j in range(m):
-                last[i, first[h] + j] = piece[:, j * N:(j + 1) * N]
+            for j, s in enumerate(columns(us)):
+                last[i, s] = piece[:, j * N:(j + 1) * N]
     for dc in range(C):
         for i in range(2):
             last_copy(i, c ^ (C - 1 - dc)).start()
 
-    for h in range(2):
-        x_end(1, h)
-        z_start(1, h)
-    total = z_end(0)
-    y_out[...] = z_end(1)
+    core_end(1, 2, 2)
+    x_copy(1, 2).wait_recv()
+    x_add(1, 2, 0, low)
+    lo_copy().start()
+    high_start(2)
 
     def y_copy():
         return remote(y_out, y_buf, ysend, yrecv, row=o)
 
+    beside = c ^ 1
+    z_wait(1, beside)
+    y_out[...] = acc[1, c, block(l, low)] + z_buf[1, beside, :low]
+    across = [(1 - side) * m + j for j in range(m)]
+
+    @pl.when(outer)
+    def _():
+        for s in across:
+            z_wait(1, s)
+            y_out[...] += z_buf[1, s, :low]
+
     y_copy().start()
-    tail = jnp.zeros((T, N), jnp.float32)
-    for i in range(2):
-        for dc in range(C):
-            s = c ^ dc
-            here = last_buf.at[i, s]
-            remote(here, here, lsend.at[0, 0], lrecv.at[i, s], row=o, col=s, layer=2 * x + i).wait_recv()
-            tail += last_buf[i, s]
-    y_copy().wait_recv()
-    total += y_buf[...]
-    o_ref[:body] = total[:body]
-    o_ref[body:] = total[body:] + tail
 
     for q in range(Kr):
-        row_a(q).wait_send()
+        for j in range(m):
+            row_a(q, j).wait_send()
         for d in range(2):
             for j in range(m):
                 b, cp = col_a(d, j, q)
@@ -617,19 +695,52 @@
     for g in range(len(groups)):
         row_i(g).wait_send()
     for d in range(2):
-        for h in range(2):
-            for keep in range(2):
-                core_copy(d, h, keep).wait_send()
-            x_copy(d, h).wait_send()
-            for j in range(m):
-                s, cp = z_copy(d, h, j)
+        for u in range(3):
+            for keep in range(2 + d):
+                core_copy(d, u, keep).wait_send()
+            x_copy(d, u).wait_send()
+
+    total = acc[0, c, block(l)]
+    for s in [beside] + across:
+        z_wait(0, s)
+        total += z_buf[0, s]
+    y_copy().wait_recv()
+    o_ref[:low] = total[:low] + y_buf[...]
+
+    @pl.when(inner)
+    def _():
+        for j in range(m):
+            here = lo_buf.at[j]
+            remote(here, here, hsend.at[1, 0], hrecv.at[1, j], row=o, col=across[j]).wait_recv()
+            o_ref[:low] += lo_buf[j]
+
+    high = total[low:]
+    for s in range(C):
+        here = hi_buf.at[s]
+        remote(here, here, hsend.at[0, 0], hrecv.at[0, s], row=o, col=s).wait_recv()
+        high += hi_buf[s]
+    tail = jnp.zeros((T, N), jnp.float32)
+    for i in range(2):
+        for s in range(C):
+            here = last_buf.at[i, s]
+            remote(here, here, lsend.at[0, 0], lrecv.at[i, s], row=o, col=s, layer=2 * x + i).wait_recv()
+            tail += last_buf[i, s]
+    o_ref[low:body] = high[:body - low]
+    o_ref[body:] = high[body - low:] + tail
+
+    for d in range(2):
+        for u in range(3 - d):
+            for j in range(units[u][1]):
+                s, cp = z_copy(d, u, j)
 
                 @pl.when(s != c)
                 def _():
                     cp.wait_send()
     for s in range(C):
+        hi_copy(s).wait_send()
         for i in range(2):
             last_copy(i, s).wait_send()
+    lo_copy().wait_send()
     y_copy().wait_send()
 
 
@@ -640,6 +751,7 @@
     Kr = K // R
     m = C // R
     T = 16
+    low = rows // 2 // 16 * 16
     dma = pltpu.SemaphoreType.DMA
     f32, bf16 = jnp.float32, jnp.bfloat16
     anyspace = pl.BlockSpec(memory_space=pl.ANY)
@@ -656,20 +768,23 @@
             pltpu.VMEM((2, M, Kr * V), bf16),
             pltpu.VMEM((2, C, M, N), f32),
             pltpu.VMEM((2, C, T, N), f32),
-            pltpu.VMEM((2, 2, 2, m, rows, N), f32),
-            pltpu.VMEM((2, 2, m, rows, N), f32),
+            pltpu.VMEM((2, 3, 2, m, rows, N), f32),
+            pltpu.VMEM((2, 3, m, rows, N), f32),
             pltpu.VMEM((2, C, rows, N), f32),
-            pltpu.VMEM((rows, N), f32),
-            pltpu.VMEM((rows, N), f32),
+            pltpu.VMEM((low, N), f32),
+            pltpu.VMEM((low, N), f32),
             pltpu.VMEM((2, C, T, N), f32),
+            pltpu.VMEM((C, rows - low, N), f32),
+            pltpu.VMEM((m, low, N), f32),
             dma((Kr,)), dma((K,)),
-            dma((Kr,)), dma((Kr,)),
-            dma((6,)), dma((6,)),
+            dma((Kr, m)), dma((Kr, m)),
+            dma((8,)), dma((8,)),
             dma((2, m, Kr)), dma((C, Kr)),
-            dma((2, 2, 2)), dma((2, 2, 2)),
-            dma((2, 2)), dma((2, 2)),
-            dma((2, 2, m)), dma((2, C)),
+            dma((2, 3, 3)), dma((2, 3, 3)),
+            dma((2, 3)), dma((2, 3)),
+            dma((2, 3, m)), dma((2, C)),
             dma, dma,
+            dma((2, C)), dma((2, C)),
             dma((2, C)), dma((2, C)),
             pltpu.SemaphoreType.REGULAR((2, C)),
         ],

time: 78.5 us -> 75 us (0.955)
  Pallas kernels: 76.7 us -> 73.2 us
    pallas_call x1, Pallas kernels: 76.7 us -> 73.2 us  [swift_call(): pl.pallas_call(functools.partial(swift, R, C, L, T), out_shape=jax.ShapeD...]
where the time goes in v2:
time: 75 us; the launch traced here: 74.8 us
  Pallas kernels  73.2 us (98%)
  other arithmetic  1.51 us (2%)
    pallas_call x1, Pallas kernels, swift_call(): pl.pallas_call(functools.partial(swift, R, C, L, T), out_shape=jax.ShapeD...  73.2 us
    div x1, other arithmetic, local(): return (coulomb.astype(jnp.float32) + own_rows) / gap_sum  1.51 us

profile of v2, /device:TPU:0, one launch (start us, length us, event | category | flops | bytes accessed | tf_op | source)
XLA Modules:
  0.0 74.8 jit_solution(5177269938503641756)
XLA Ops:
  0.0 0.0 copy-start.1
  0.0 0.0 copy-start.2
  0.0 0.0 copy-start
  0.0 73.2 %shard_map.55 = f32[96,128]{1,0:T(8,128)} custom-call(bf16[16,256,384]{2,1,0:T(8,128)(2,1)} %i_ref.1, bf16[16,512,128]{2,1,0:T(8,128)(2,1)} %a_ref.1), custom_call_target="tpu_custom_call" | custom-call | tf_op jit(solution)/shard_map/pallas_call | solution.py:758
  73.3 0.0 copy-done.1
  73.3 0.0 copy-done.2
  73.3 0.0 copy-done
  73.3 1.5 %add_divide_fusion = f32[96,128]{1,0:T(8,128)} fusion(f32[96,128]{1,0:T(8,128)} %shard_map.55, bf16[96,128]{1,0:T(8,128)(2,1)S(1)} %copy-done, f32[128]{0:T(128)S(1)} %copy-done.1, f32[96]{0:T(128)S(1)} %copy-done.2), kind=kLoop, calls=%fused_computation | loop fusion | flops 49152 | bytes 123776 | tf_op jit(solution)/shard_map/div | solution.py:800
Async XLA Ops:
  0.0 73.3 %copy-start.1 = (f32[128]{0:T(128)S(1)}, f32[128]{0:T(128)}, u32[]{:S(2)}) copy-start(f32[128]{0:T(128)} %param.9) | copy-start | bytes 1540
  0.0 73.3 %copy-start.2 = (f32[96]{0:T(128)S(1)}, f32[96]{0:T(128)}, u32[]{:S(2)}) copy-start(f32[96]{0:T(128)} %param.8) | copy-start | bytes 1156
  0.0 73.3 %copy-start = (bf16[96,128]{1,0:T(8,128)(2,1)S(1)}, bf16[96,128]{1,0:T(8,128)(2,1)}, u32[]{:S(2)}) copy-start(bf16[96,128]{1,0:T(8,128)(2,1)} %param.7) | copy-start | bytes 73732

commit v3 on v0

--- a/solution.py
+++ b/solution.py
@@ -265,7 +265,7 @@
         col_sum(dc).wait_send()
 
 
-def local(R, C, L, integrals, amplitudes, coulomb, row_gap, col_gap):
+def general_call(R, C, L, integrals, amplitudes):
     K, V, M = integrals.shape
     V_row, N = amplitudes.shape[1:]
     rows = M // L
@@ -276,7 +276,7 @@
     dma = pltpu.SemaphoreType.DMA
     vmem = pl.BlockSpec(memory_space=pltpu.VMEM)
     anyspace = pl.BlockSpec(memory_space=pl.ANY)
-    own_rows = pl.pallas_call(
+    return pl.pallas_call(
         functools.partial(kernel, R, C, L, Q),
         out_shape=jax.ShapeDtypeStruct((rows, N), jnp.float32),
         in_specs=[anyspace, anyspace],
@@ -300,6 +300,453 @@
         ],
         compiler_params=pltpu.CompilerParams(collective_id=0, has_side_effects=True),
     )(integrals, amplitudes)
+
+
+def swift(R, C, L, T, lo, i_ref, a_ref, o_ref,
+          a_x, az, i_in, i_s, i_t, acc, last, core_buf, x_buf, z_buf, y_out, y_buf, last_buf, hi_buf, lo_buf,
+          own, iown, asend, arecv, isend, irecv, zsend, zrecv,
+          csend, crecv, xsend, xrecv, wsend, wrecv, ysend, yrecv, lsend, lrecv, hsend, hrecv, there):
+    r, c, l = lax.axis_index("row"), lax.axis_index("col"), lax.axis_index("layer")
+    K, V, M = i_ref.shape
+    N = a_ref.shape[2]
+    Kr = K // R
+    W = Kr * V
+    m = C // R
+    rows = M // L
+    half_rows = 2 * rows
+    o = 1 - r
+    x, core = lax.div(l, 2), lax.rem(l, 2)
+    side = lax.div(c, m)
+    home = side == r
+    away = jnp.logical_not(home)
+    outer = (c == 0) | (c == C - 1)
+    inner = jnp.logical_not(outer)
+
+    def remote(src, dst, ss, rs, **to):
+        where = {"row": r, "col": c, "layer": l}
+        where.update(to)
+        return pltpu.make_async_remote_copy(src_ref=src, dst_ref=dst, send_sem=ss, recv_sem=rs,
+                                            device_id=where, device_id_type=MESH)
+
+    def landed(ref, sem):
+        pltpu.make_async_copy(ref, ref, sem).wait()
+
+    def signal(sem, **to):
+        where = {"row": r, "col": c, "layer": l}
+        where.update(to)
+        pl.semaphore_signal(sem, inc=1, device_id=where, device_id_type=MESH)
+
+    def at(start, size, unit=16):
+        return pl.ds(pl.multiple_of(start, unit), size)
+
+    sib, opp = l ^ 1, l ^ 2
+
+    barrier = pltpu.get_barrier_semaphore()
+    signal(barrier, row=o)
+    signal(barrier, layer=sib)
+    signal(barrier, layer=opp)
+
+    @pl.when(c > 0)
+    def _():
+        signal(barrier, col=c - 1)
+
+    @pl.when(c < C - 1)
+    def _():
+        signal(barrier, col=c + 1)
+
+    pl.semaphore_wait(barrier, 3 + (c > 0).astype(jnp.int32) + (c < C - 1).astype(jnp.int32))
+
+    def row_a(q, j):
+        span = pl.ds(j * V, V)
+        return remote(a_ref.at[o * Kr + q, span], a_x.at[q, span], asend, arecv.at[q, j], row=o)
+
+    for q in range(Kr):
+        for j in range(m):
+            row_a(q, j).start()
+
+    def col_start(d, *qs, js=range(m)):
+        for q in qs:
+            for j in js:
+                b = (o if d else r) * m + j
+                span = pl.ds(j * V, V)
+                src = a_x.at[q, span] if d else a_ref.at[r * Kr + q, span]
+
+                @pl.when(b != c)
+                def _():
+                    remote(src, az.at[c, q], zsend, zrecv.at[c], col=b).start()
+
+    ahead, turnover = 3, Kr - 2
+
+    @pl.when(home)
+    def _():
+        col_start(0, *range(ahead))
+
+    @pl.when(home & inner)
+    def _():
+        col_start(0, *range(ahead, Kr))
+
+    for t in range(2, C):
+        @pl.when((c >= 1) & (c + t - 1 < C))
+        def _():
+            signal(there.at[0, t - 2], col=c - 1)
+
+        @pl.when((c + 1 < C) & (c - t + 1 >= 0))
+        def _():
+            signal(there.at[1, t - 2], col=c + 1)
+
+        @pl.when(c + t < C)
+        def _():
+            pl.semaphore_wait(there.at[0, t - 2], 1)
+
+        @pl.when(c - t >= 0)
+        def _():
+            pl.semaphore_wait(there.at[1, t - 2], 1)
+
+    @pl.when(away & outer)
+    def _():
+        col_start(0, *range(Kr))
+
+    here_v = at(lax.rem(c, m) * V, V, V)
+
+    def own_a(q, src):
+        pltpu.make_async_copy(src.at[q, here_v], az.at[c, q], own).start()
+
+    per = 2
+
+    def own_k(n):
+        return (r if n * per >= Kr else o) * Kr + n * per % Kr
+
+    for n in range(K // per):
+        pltpu.make_async_copy(i_ref.at[pl.ds(own_k(n), per)], i_in.at[pl.ds(n * per, per)], iown.at[n]).start()
+
+    @pl.when(home)
+    def _():
+        for q in range(Kr):
+            pltpu.make_async_copy(a_ref.at[r * Kr + q, here_v], az.at[c, q], own).start()
+
+    other = (1 - x) * half_rows
+    mine = x * half_rows
+    first, middle, final = (T, lo - T), (lo, rows - lo), (0, T)
+
+    def both(part):
+        start, size = part
+        return [(mine + start, size), (mine + rows + start, size)]
+
+    groups = [(other, half_rows)] + both(first) + both(middle) + both(final)
+
+    def row_i(g):
+        start, size = groups[g]
+        span = at(start, size)
+        return remote(i_s.at[span], i_t.at[1, span], isend, irecv.at[(g + 1) // 2], row=o)
+
+    def slab_wait(n):
+        size = groups[2 * n - 1][1] * 2 if n else half_rows
+        landed(i_t.at[1, pl.ds(0, size)], irecv.at[n])
+
+    for q in range(Kr):
+        for j in range(m):
+            row_a(q, j).wait_recv()
+            if q < turnover:
+                @pl.when(outer | away)
+                def _():
+                    col_start(1, q, js=[j])
+            else:
+                col_start(1, q, js=[j])
+
+        @pl.when(away)
+        def _():
+            own_a(q, a_x)
+
+        if q == turnover:
+            @pl.when(inner & home)
+            def _():
+                col_start(1, *range(turnover))
+
+            @pl.when(inner & away)
+            def _():
+                col_start(0, *range(Kr))
+
+            @pl.when(outer & home)
+            def _():
+                col_start(0, *range(ahead, Kr))
+
+        if q < K // per:
+            landed(i_in.at[pl.ds(q * per, per)], iown.at[q])
+            for k in range(q * per, q * per + per):
+                if k < Kr:
+                    i_s[:, k * V:(k + 1) * V] = i_in[k].T
+                else:
+                    i_t[0, :, (k - Kr) * V:(k - Kr + 1) * V] = i_in[k].T
+            if (q + 1) * per == Kr:
+                for g in range(len(groups)):
+                    row_i(g).start()
+
+    cols = [side * m, side * m + 1, (1 - side) * (C - 1), 2 - side]
+    near, wide, late = (0, 2), (2, 1), (3, 1)
+    early = (0, 3)
+
+    def pick(u):
+        return cols[u[0]:u[0] + u[1]]
+
+    def wait_piece(s):
+        @pl.when(s == c)
+        def _():
+            landed(az.at[c], own)
+
+        @pl.when(s != c)
+        def _():
+            landed(az.at[s], zrecv.at[s])
+
+    def fill(d, u, spans, keep=None):
+        left = [i_t[d, at(start, size)] for start, size in spans]
+        left = left[0] if len(left) == 1 else jnp.concatenate(left, axis=0)
+        right = [az[s].reshape(W, N) for s in pick(u)]
+        right = right[0] if len(right) == 1 else jnp.concatenate(right, axis=1)
+        piece = lax.dot_general(left, right, (((1,), (0,)), ((), ())), preferred_element_type=jnp.float32)
+        for j, s in enumerate(pick(u)):
+            done = 0
+            for i, (start, size) in enumerate(spans):
+                part = piece[done:done + size, j * N:(j + 1) * N]
+                if keep is None:
+                    acc[d, s, at(start, size)] = part
+                else:
+                    keep[i, s] = part
+                done += size
+
+    def from_to(u):
+        return pl.ds(cols[u[0]], u[1]), pl.ds(u[0], u[1])
+
+    def core_span(d, keep):
+        return first if d and keep == 1 else middle if keep == 2 else (0, rows)
+
+    def core_start(d, us, keep):
+        start, size = core_span(d, keep)
+        give = 2 * (x if keep else 1 - x) + 1 - core
+        for u in us:
+            src, dst = from_to(u)
+            remote(acc.at[d, src, at(give * rows + start, size)], core_buf.at[d, min(keep, 1), dst, pl.ds(start, size)],
+                   csend, crecv.at[d, us[0][0] // 3, keep], layer=sib).start()
+
+    def core_end(d, us, keep):
+        start, size = core_span(d, keep)
+        have = 2 * (x if keep else 1 - x) + core
+        slots = pl.ds(us[0][0], sum(u[1] for u in us))
+        landed(core_buf.at[d, min(keep, 1), slots, pl.ds(start, size)], crecv.at[d, us[0][0] // 3, keep])
+        for u in us:
+            src, dst = from_to(u)
+            acc[d, src, at(have * rows + start, size)] += core_buf[d, min(keep, 1), dst, start:start + size]
+
+    def x_start(d, us):
+        for u in us:
+            src, dst = from_to(u)
+            remote(acc.at[d, src, at((2 * (1 - x) + core) * rows, rows)], x_buf.at[d, dst],
+                   xsend, xrecv.at[d, us[0][0] // 3], layer=opp).start()
+
+    def x_wait(d, us):
+        landed(x_buf.at[d, pl.ds(us[0][0], sum(u[1] for u in us))], xrecv.at[d, us[0][0] // 3])
+
+    def x_add(d, us, start, size, add=True):
+        for u in us:
+            src, dst = from_to(u)
+            where = at(l * rows + start, size)
+            if add:
+                acc[d, src, where] += x_buf[d, dst, start:start + size]
+            else:
+                acc[d, src, where] = x_buf[d, dst, start:start + size]
+
+    def z_start(d, u):
+        size = lo if d else rows
+        for s in pick(u):
+            slot = (c ^ s) - 1
+            sem = wrecv.at[jnp.where(slot == 0, 1, 2)] if d else wrecv.at[0]
+
+            @pl.when(s != c)
+            def _():
+                remote(acc.at[d, s, at(l * rows, size)], z_buf.at[d, slot, pl.ds(0, size)], wsend, sem, col=s).start()
+
+    def hi_start(us):
+        for u in us:
+            for s in pick(u):
+                remote(acc.at[1, s, at(l * rows + lo, rows - lo)], hi_buf.at[c], hsend, hrecv.at[0], row=o, col=s).start()
+
+    def lo_start():
+        s = cols[3]
+        remote(acc.at[1, s, at(l * rows, lo)], lo_buf.at[lax.rem(c, m)], hsend, hrecv.at[1], row=o, col=s).start()
+
+    most = (near, wide)
+    for i in range(3):
+        wait_piece(cols[i])
+    for u in most:
+        fill(0, u, [(0, M)])
+    core_start(0, most, 0)
+    core_start(0, most, 1)
+    core_end(0, most, 0)
+    x_start(0, most)
+    core_end(0, most, 1)
+
+    slab_wait(0)
+    for u in most:
+        fill(1, u, [(other, half_rows)])
+    core_start(1, most, 0)
+    x_wait(0, most)
+    x_add(0, most, 0, rows)
+    z_start(0, near)
+    core_end(1, most, 0)
+    x_start(1, most)
+
+    wait_piece(cols[3])
+    fill(0, late, [(other, half_rows)])
+    core_start(0, [late], 0)
+    fill(1, late, [(other, half_rows)])
+    core_start(1, [late], 0)
+    z_start(0, wide)
+    core_end(0, [late], 0)
+    x_start(0, [late])
+    core_end(1, [late], 0)
+    x_start(1, [late])
+    fill(0, late, [(mine, half_rows)])
+    core_start(0, [late], 1)
+
+    slab_wait(1)
+    for u in (near, (2, 2)):
+        fill(1, u, both(first))
+    core_start(1, most, 1)
+    core_start(1, [late], 1)
+    x_wait(1, most)
+    core_end(0, [late], 1)
+    core_end(1, most, 1)
+    x_add(1, most, 0, T, add=False)
+    x_add(1, most, T, lo - T)
+    z_start(1, near)
+    z_start(1, wide)
+    core_end(1, [late], 1)
+    x_wait(0, [late])
+    x_add(0, [late], 0, rows)
+    z_start(0, late)
+
+    slab_wait(2)
+    for u in (near, (2, 2)):
+        fill(1, u, both(middle))
+    core_start(1, most, 2)
+    core_start(1, [late], 2)
+    x_wait(1, [late])
+    x_add(1, [late], 0, T, add=False)
+    x_add(1, [late], T, lo - T)
+    lo_start()
+    core_end(1, most, 2)
+    x_add(1, most, lo, rows - lo)
+    hi_start(most)
+    core_end(1, [late], 2)
+    x_add(1, [late], lo, rows - lo)
+    hi_start([late])
+
+    slab_wait(3)
+    for u in (near, (2, 2)):
+        fill(1, u, both(final), keep=last)
+    for dc in range(C):
+        s = c ^ (C - 1 - dc)
+        for i in range(2):
+            remote(last.at[i, s], last_buf.at[core, c], lsend, lrecv, row=o, col=s, layer=2 * x + i).start()
+
+    landed(z_buf.at[1, 0, pl.ds(0, lo)], wrecv.at[1])
+    y_out[...] = acc[1, c, at(l * rows, lo)] + z_buf[1, 0, :lo]
+
+    @pl.when(outer)
+    def _():
+        landed(z_buf.at[1, pl.ds(1, 2), pl.ds(0, lo)], wrecv.at[2])
+        y_out[...] += z_buf[1, 1, :lo] + z_buf[1, 2, :lo]
+
+    remote(y_out, y_buf, ysend, yrecv, row=o).start()
+
+    landed(a_x, asend)
+    landed(az.at[pl.ds(0, m + 1)], zsend)
+    landed(i_s, isend)
+    landed(acc.at[0, :, pl.ds(0, M - T)], csend)
+    landed(acc.at[0, :, pl.ds(0, half_rows)], xsend)
+
+    landed(z_buf.at[0], wrecv.at[0])
+    total = acc[0, c, at(l * rows, rows)]
+    for i in range(C - 1):
+        total += z_buf[0, i]
+    landed(y_buf, yrecv)
+    o_ref[:lo] = total[:lo] + y_buf[...]
+
+    @pl.when(inner)
+    def _():
+        landed(lo_buf, hrecv.at[1])
+        o_ref[:lo] += lo_buf[0] + lo_buf[1]
+
+    landed(hi_buf, hrecv.at[0])
+    high = total[lo:]
+    for s in range(C):
+        high += hi_buf[s]
+    o_ref[lo:] = high
+    landed(last_buf, lrecv)
+    tail = o_ref[:T]
+    for i in range(2):
+        for s in range(C):
+            tail += last_buf[i, s]
+    o_ref[:T] = tail
+
+    landed(acc.at[0, 0, pl.ds(0, 3 * rows + 2 * lo)] if 3 * rows + 2 * lo <= M else acc.at[0, pl.ds(0, 2), pl.ds(0, (3 * rows + 2 * lo) // 2)],
+           wsend)
+    landed(acc.at[0, 0, pl.ds(0, C * (rows - lo) + lo)], hsend)
+    landed(last, lsend)
+    landed(y_out, ysend)
+
+
+def swift_call(R, C, L, integrals, amplitudes):
+    K, V, M = integrals.shape
+    V_row, N = amplitudes.shape[1:]
+    rows = M // L
+    Kr = K // R
+    m = C // R
+    T = 16
+    lo = rows * 5 // 6 // 16 * 16
+    dma = pltpu.SemaphoreType.DMA
+    f32, bf16 = jnp.float32, jnp.bfloat16
+    anyspace = pl.BlockSpec(memory_space=pl.ANY)
+    return pl.pallas_call(
+        functools.partial(swift, R, C, L, T, lo),
+        out_shape=jax.ShapeDtypeStruct((rows, N), f32),
+        in_specs=[anyspace, anyspace],
+        out_specs=pl.BlockSpec(memory_space=pltpu.VMEM),
+        scratch_shapes=[
+            pltpu.VMEM((Kr, V_row, N), bf16),
+            pltpu.VMEM((C, Kr, V, N), bf16),
+            pltpu.VMEM((K, V, M), bf16),
+            pltpu.VMEM((M, Kr * V), bf16),
+            pltpu.VMEM((2, M, Kr * V), bf16),
+            pltpu.VMEM((2, C, M, N), f32),
+            pltpu.VMEM((2, C, T, N), f32),
+            pltpu.VMEM((2, 2, C, rows, N), f32),
+            pltpu.VMEM((2, C, rows, N), f32),
+            pltpu.VMEM((2, C - 1, rows, N), f32),
+            pltpu.VMEM((lo, N), f32),
+            pltpu.VMEM((lo, N), f32),
+            pltpu.VMEM((2, C, T, N), f32),
+            pltpu.VMEM((C, rows - lo, N), f32),
+            pltpu.VMEM((m, lo, N), f32),
+            dma, dma((Kr,)),
+            dma, dma((Kr, m)),
+            dma, dma((4,)),
+            dma, dma((C,)),
+            dma, dma((2, 2, 3)),
+            dma, dma((2, 2)),
+            dma, dma((3,)),
+            dma, dma,
+            dma, dma,
+            dma, dma((2,)),
+            pltpu.SemaphoreType.REGULAR((2, C - 2)),
+        ],
+        compiler_params=pltpu.CompilerParams(collective_id=0, has_side_effects=True),
+    )(integrals, amplitudes)
+
+
+def local(R, C, L, integrals, amplitudes, coulomb, row_gap, col_gap):
+    swift_fits = R == 2 and C == 4 and L == 4 and integrals.shape[2] % (16 * L) == 0
+    call = swift_call if swift_fits else general_call
+    own_rows = call(R, C, L, integrals, amplitudes)
     gap_sum = row_gap[:, None] + col_gap[None, :]
     return (coulomb.astype(jnp.float32) + own_rows) / gap_sum
 

time: 78.6 us -> 72.1 us (0.917)
  Pallas kernels: 76.9 us -> 70.4 us
    pallas_call x1, Pallas kernels: 76.9 us -> 70.4 us  [swift_call(): pl.pallas_call(functools.partial(swift, R, C, L, T, lo), out_shape=jax.Sh...]
where the time goes in v3:
time: 72.1 us; the launch traced here: 72 us
  Pallas kernels  70.4 us (98%)
  other arithmetic  1.51 us (2%)
    pallas_call x1, Pallas kernels, swift_call(): pl.pallas_call(functools.partial(swift, R, C, L, T, lo), out_shape=jax.Sh...  70.4 us
    div x1, other arithmetic, local(): return (coulomb.astype(jnp.float32) + own_rows) / gap_sum  1.51 us

profile of v3, /device:TPU:0, one launch (start us, length us, event | category | flops | bytes accessed | tf_op | source)
XLA Modules:
  0.0 72.0 jit_solution(2177832905743933987)
XLA Ops:
  0.0 0.0 copy-start.1
  0.0 0.0 copy-start.2
  0.0 0.0 copy-start
  0.0 70.4 %shard_map.55 = f32[96,128]{1,0:T(8,128)} custom-call(bf16[16,256,384]{2,1,0:T(8,128)(2,1)} %i_ref.1, bf16[16,512,128]{2,1,0:T(8,128)(2,1)} %a_ref.1), custom_call_target="tpu_custom_call" | custom-call | tf_op jit(solution)/shard_map/pallas_call | solution.py:709
  70.4 0.0 copy-done.1
  70.4 0.0 copy-done.2
  70.4 0.0 copy-done
  70.5 1.5 %add_divide_fusion = f32[96,128]{1,0:T(8,128)} fusion(f32[96,128]{1,0:T(8,128)} %shard_map.55, bf16[96,128]{1,0:T(8,128)(2,1)S(1)} %copy-done, f32[128]{0:T(128)S(1)} %copy-done.1, f32[96]{0:T(128)S(1)} %copy-done.2), kind=kLoop, calls=%fused_computation | loop fusion | flops 49152 | bytes 123776 | tf_op jit(solution)/shard_map/div | solution.py:751
Async XLA Ops:
  0.0 70.4 %copy-start.1 = (f32[128]{0:T(128)S(1)}, f32[128]{0:T(128)}, u32[]{:S(2)}) copy-start(f32[128]{0:T(128)} %param.9) | copy-start | bytes 1540
  0.0 70.4 %copy-start.2 = (f32[96]{0:T(128)S(1)}, f32[96]{0:T(128)}, u32[]{:S(2)}) copy-start(f32[96]{0:T(128)} %param.8) | copy-start | bytes 1156
  0.0 70.4 %copy-start = (bf16[96,128]{1,0:T(8,128)(2,1)S(1)}, bf16[96,128]{1,0:T(8,128)(2,1)}, u32[]{:S(2)}) copy-start(bf16[96,128]{1,0:T(8,128)(2,1)} %param.7) | copy-start | bytes 73732

commit v4 on v3

--- a/solution.py
+++ b/solution.py
@@ -303,9 +303,9 @@
 
 
 def swift(R, C, L, T, lo, i_ref, a_ref, o_ref,
-          a_x, az, i_in, i_s, i_t, acc, last, core_buf, x_buf, z_buf, y_out, y_buf, last_buf, hi_buf, lo_buf,
+          a_x, az, i_in, i_s, i_t, acc, last, core_buf, x_buf, p_buf, z_buf, y_out, y_buf, last_buf, hi_buf, lo_buf,
           own, iown, asend, arecv, isend, irecv, zsend, zrecv,
-          csend, crecv, xsend, xrecv, wsend, wrecv, ysend, yrecv, lsend, lrecv, hsend, hrecv, there):
+          csend, crecv, xsend, xrecv, wsend, precv, wrecv, ysend, yrecv, lsend, lrecv, hsend, hrecv, there):
     r, c, l = lax.axis_index("row"), lax.axis_index("col"), lax.axis_index("layer")
     K, V, M = i_ref.shape
     N = a_ref.shape[2]
@@ -375,7 +375,7 @@
                 def _():
                     remote(src, az.at[c, q], zsend, zrecv.at[c], col=b).start()
 
-    ahead, turnover = 3, Kr - 2
+    ahead, hold, turnover = 3, 2, Kr - 2
 
     @pl.when(home)
     def _():
@@ -402,9 +402,13 @@
         def _():
             pl.semaphore_wait(there.at[1, t - 2], 1)
 
+    @pl.when(away)
+    def _():
+        col_start(0, *range(hold))
+
     @pl.when(away & outer)
     def _():
-        col_start(0, *range(Kr))
+        col_start(0, *range(hold, Kr))
 
     here_v = at(lax.rem(c, m) * V, V, V)
 
@@ -446,7 +450,7 @@
     for q in range(Kr):
         for j in range(m):
             row_a(q, j).wait_recv()
-            if q < turnover:
+            if hold <= q < turnover:
                 @pl.when(outer | away)
                 def _():
                     col_start(1, q, js=[j])
@@ -460,11 +464,11 @@
         if q == turnover:
             @pl.when(inner & home)
             def _():
-                col_start(1, *range(turnover))
+                col_start(1, *range(hold, turnover))
 
             @pl.when(inner & away)
             def _():
-                col_start(0, *range(Kr))
+                col_start(0, *range(hold, Kr))
 
             @pl.when(outer & home)
             def _():
@@ -554,15 +558,22 @@
             else:
                 acc[d, src, where] = x_buf[d, dst, start:start + size]
 
-    def z_start(d, u):
-        size = lo if d else rows
-        for s in pick(u):
-            slot = (c ^ s) - 1
-            sem = wrecv.at[jnp.where(slot == 0, 1, 2)] if d else wrecv.at[0]
-
-            @pl.when(s != c)
-            def _():
-                remote(acc.at[d, s, at(l * rows, size)], z_buf.at[d, slot, pl.ds(0, size)], wsend, sem, col=s).start()
+    def z_start(d, s):
+        size, slot = lo if d else rows, (c ^ s) - 1
+        sem = wrecv.at[d, jnp.where(slot == 0, 0, 1)]
+        remote(acc.at[d, s, at(l * rows, size)], z_buf.at[d, slot, pl.ds(0, size)], wsend, sem, col=s).start()
+
+    def lean(d, s):
+        @pl.when(outer)
+        def _():
+            remote(acc.at[d, s, at(l * rows, rows)], p_buf, wsend, precv, col=c ^ 1).start()
+
+    def across(d, s):
+        @pl.when(inner)
+        def _():
+            landed(p_buf, precv)
+            acc[d, s, at(l * rows, rows)] += p_buf[...]
+            z_start(d, s)
 
     def hi_start(us):
         for u in us:
@@ -590,7 +601,8 @@
     core_start(1, most, 0)
     x_wait(0, most)
     x_add(0, most, 0, rows)
-    z_start(0, near)
+    z_start(0, c ^ 1)
+    lean(0, cols[2])
     core_end(1, most, 0)
     x_start(1, most)
 
@@ -599,7 +611,7 @@
     core_start(0, [late], 0)
     fill(1, late, [(other, half_rows)])
     core_start(1, [late], 0)
-    z_start(0, wide)
+    across(0, cols[2])
     core_end(0, [late], 0)
     x_start(0, [late])
     core_end(1, [late], 0)
@@ -612,27 +624,27 @@
         fill(1, u, both(first))
     core_start(1, most, 1)
     core_start(1, [late], 1)
+    core_end(0, [late], 1)
+    x_wait(0, [late])
+    x_add(0, [late], 0, rows)
+    z_start(0, cols[3])
     x_wait(1, most)
-    core_end(0, [late], 1)
     core_end(1, most, 1)
     x_add(1, most, 0, T, add=False)
     x_add(1, most, T, lo - T)
-    z_start(1, near)
-    z_start(1, wide)
+    z_start(1, cols[2])
+    z_start(1, c ^ 1)
     core_end(1, [late], 1)
-    x_wait(0, [late])
-    x_add(0, [late], 0, rows)
-    z_start(0, late)
+    x_wait(1, [late])
+    x_add(1, [late], 0, T, add=False)
+    x_add(1, [late], T, lo - T)
+    lo_start()
 
     slab_wait(2)
     for u in (near, (2, 2)):
         fill(1, u, both(middle))
     core_start(1, most, 2)
     core_start(1, [late], 2)
-    x_wait(1, [late])
-    x_add(1, [late], 0, T, add=False)
-    x_add(1, [late], T, lo - T)
-    lo_start()
     core_end(1, most, 2)
     x_add(1, most, lo, rows - lo)
     hi_start(most)
@@ -648,12 +660,12 @@
         for i in range(2):
             remote(last.at[i, s], last_buf.at[core, c], lsend, lrecv, row=o, col=s, layer=2 * x + i).start()
 
-    landed(z_buf.at[1, 0, pl.ds(0, lo)], wrecv.at[1])
+    landed(z_buf.at[1, 0, pl.ds(0, lo)], wrecv.at[1, 0])
     y_out[...] = acc[1, c, at(l * rows, lo)] + z_buf[1, 0, :lo]
 
     @pl.when(outer)
     def _():
-        landed(z_buf.at[1, pl.ds(1, 2), pl.ds(0, lo)], wrecv.at[2])
+        landed(z_buf.at[1, pl.ds(1, 2), pl.ds(0, lo)], wrecv.at[1, 1])
         y_out[...] += z_buf[1, 1, :lo] + z_buf[1, 2, :lo]
 
     remote(y_out, y_buf, ysend, yrecv, row=o).start()
@@ -664,20 +676,23 @@
     landed(acc.at[0, :, pl.ds(0, M - T)], csend)
     landed(acc.at[0, :, pl.ds(0, half_rows)], xsend)
 
-    landed(z_buf.at[0], wrecv.at[0])
-    total = acc[0, c, at(l * rows, rows)]
-    for i in range(C - 1):
-        total += z_buf[0, i]
-    landed(y_buf, yrecv)
-    o_ref[:lo] = total[:lo] + y_buf[...]
+    landed(z_buf.at[0, 0], wrecv.at[0, 0])
+    o_ref[...] = acc[0, c, at(l * rows, rows)] + z_buf[0, 0]
+
+    @pl.when(outer)
+    def _():
+        landed(z_buf.at[0, 0], wrecv.at[0, 1])
+        o_ref[...] += z_buf[0, 1]
 
     @pl.when(inner)
     def _():
+        landed(z_buf.at[0, pl.ds(1, 2)], wrecv.at[0, 1])
+        o_ref[...] += z_buf[0, 1] + z_buf[0, 2]
         landed(lo_buf, hrecv.at[1])
         o_ref[:lo] += lo_buf[0] + lo_buf[1]
 
     landed(hi_buf, hrecv.at[0])
-    high = total[lo:]
+    high = o_ref[lo:]
     for s in range(C):
         high += hi_buf[s]
     o_ref[lo:] = high
@@ -687,6 +702,8 @@
         for s in range(C):
             tail += last_buf[i, s]
     o_ref[:T] = tail
+    landed(y_buf, yrecv)
+    o_ref[:lo] += y_buf[...]
 
     landed(acc.at[0, 0, pl.ds(0, 3 * rows + 2 * lo)] if 3 * rows + 2 * lo <= M else acc.at[0, pl.ds(0, 2), pl.ds(0, (3 * rows + 2 * lo) // 2)],
            wsend)
@@ -708,7 +725,7 @@
     anyspace = pl.BlockSpec(memory_space=pl.ANY)
     return pl.pallas_call(
         functools.partial(swift, R, C, L, T, lo),
-        out_shape=jax.ShapeDtypeStruct((rows, N), f32),
+        out_shape=pltpu.VMEM((rows, N), f32),
         in_specs=[anyspace, anyspace],
         out_specs=pl.BlockSpec(memory_space=pltpu.VMEM),
         scratch_shapes=[
@@ -721,6 +738,7 @@
             pltpu.VMEM((2, C, T, N), f32),
             pltpu.VMEM((2, 2, C, rows, N), f32),
             pltpu.VMEM((2, C, rows, N), f32),
+            pltpu.VMEM((rows, N), f32),
             pltpu.VMEM((2, C - 1, rows, N), f32),
             pltpu.VMEM((lo, N), f32),
             pltpu.VMEM((lo, N), f32),
@@ -733,7 +751,7 @@
             dma, dma((C,)),
             dma, dma((2, 2, 3)),
             dma, dma((2, 2)),
-            dma, dma((3,)),
+            dma, dma, dma((2, 2)),
             dma, dma,
             dma, dma,
             dma, dma((2,)),

time: 72.1 us -> 69.8 us (0.968)
  Pallas kernels: 70.4 us -> 68.8 us
  other arithmetic: 1.51 us -> 0.71 us
    pallas_call x1, Pallas kernels: 70.4 us -> 68.8 us  [swift_call(): pl.pallas_call(functools.partial(swift, R, C, L, T, lo), out_shape=pltpu....]
    div x1, other arithmetic: 1.51 us -> 0.71 us  [local(): return (coulomb.astype(jnp.float32) + own_rows) / gap_sum]
where the time goes in v4:
time: 69.8 us; the launch traced here: 69.5 us
  Pallas kernels  68.8 us (99%)
  other arithmetic  0.71 us (1%)
    pallas_call x1, Pallas kernels, swift_call(): pl.pallas_call(functools.partial(swift, R, C, L, T, lo), out_shape=pltpu....  68.8 us

profile of v4, /device:TPU:0, one launch (start us, length us, event | category | flops | bytes accessed | tf_op | source)
XLA Modules:
  0.0 69.5 jit_solution(11526503978695220624)
XLA Ops:
  0.0 0.0 copy-start.1
  0.0 0.0 copy-start.2
  0.0 0.0 copy-start
  0.0 68.8 %shard_map.55 = f32[96,128]{1,0:T(8,128)S(1)} custom-call(bf16[16,256,384]{2,1,0:T(8,128)(2,1)} %i_ref.1, bf16[16,512,128]{2,1,0:T(8,128)(2,1)} %a_ref.1), custom_call_target="tpu_custom_call" | custom-call | tf_op jit(solution)/shard_map/pallas_call | solution.py:726
  68.8 0.0 copy-done.1
  68.8 0.0 copy-done.2
  68.8 0.0 copy-done
  68.8 0.7 %add_divide_fusion = f32[96,128]{1,0:T(8,128)} fusion(f32[96,128]{1,0:T(8,128)S(1)} %shard_map.55, bf16[96,128]{1,0:T(8,128)(2,1)S(1)} %copy-done, f32[128]{0:T(128)S(1)} %copy-done.1, f32[96]{0:T(128)S(1)} %copy-done.2), kind=kLoop, calls=%fused_computation | loop fusion | flops 49152 | bytes 123776 | tf_op jit(solution)/shard_map/div | solution.py:769
Async XLA Ops:
  0.0 68.8 %copy-start.1 = (f32[128]{0:T(128)S(1)}, f32[128]{0:T(128)}, u32[]{:S(2)}) copy-start(f32[128]{0:T(128)} %param.9) | copy-start | bytes 1540
  0.0 68.8 %copy-start.2 = (f32[96]{0:T(128)S(1)}, f32[96]{0:T(128)}, u32[]{:S(2)}) copy-start(f32[96]{0:T(128)} %param.8) | copy-start | bytes 1156
  0.0 68.8 %copy-start = (bf16[96,128]{1,0:T(8,128)(2,1)S(1)}, bf16[96,128]{1,0:T(8,128)(2,1)}, u32[]{:S(2)}) copy-start(bf16[96,128]{1,0:T(8,128)(2,1)} %param.7) | copy-start | bytes 73732

commit v5 on v4

--- a/solution.py
+++ b/solution.py
@@ -303,7 +303,7 @@
 
 
 def swift(R, C, L, T, lo, i_ref, a_ref, o_ref,
-          a_x, az, i_in, i_s, i_t, acc, last, core_buf, x_buf, p_buf, z_buf, y_out, y_buf, last_buf, hi_buf, lo_buf,
+          a_x, az, i_in, i_s, i_t, acc, last, core_buf, x_buf, p_buf, z_buf, y_out, y_buf, last_buf, hi_buf,
           own, iown, asend, arecv, isend, irecv, zsend, zrecv,
           csend, crecv, xsend, xrecv, wsend, precv, wrecv, ysend, yrecv, lsend, lrecv, hsend, hrecv, there):
     r, c, l = lax.axis_index("row"), lax.axis_index("col"), lax.axis_index("layer")
@@ -432,20 +432,14 @@
     mine = x * half_rows
     first, middle, final = (T, lo - T), (lo, rows - lo), (0, T)
 
-    def both(part):
-        start, size = part
-        return [(mine + start, size), (mine + rows + start, size)]
-
-    groups = [(other, half_rows)] + both(first) + both(middle) + both(final)
+    parts = (final, first, middle)
+    order = [(i * rows + start, size) for start, size in parts for i in range(2)]
+    place = {part: 2 * part[0] for part in parts}
+    slabs = [(other, half_rows)] + [(mine + place[part], 2 * part[1]) for part in (first, middle, final)]
 
     def row_i(g):
-        start, size = groups[g]
-        span = at(start, size)
-        return remote(i_s.at[span], i_t.at[1, span], isend, irecv.at[(g + 1) // 2], row=o)
-
-    def slab_wait(n):
-        size = groups[2 * n - 1][1] * 2 if n else half_rows
-        landed(i_t.at[1, pl.ds(0, size)], irecv.at[n])
+        span = at(*slabs[g])
+        return remote(i_s.at[span], i_t.at[1, span], isend, irecv.at[g], row=o)
 
     for q in range(Kr):
         for j in range(m):
@@ -478,11 +472,22 @@
             landed(i_in.at[pl.ds(q * per, per)], iown.at[q])
             for k in range(q * per, q * per + per):
                 if k < Kr:
-                    i_s[:, k * V:(k + 1) * V] = i_in[k].T
+                    turned = i_in[k].T
+                    for i in range(2):
+                        half = turned[i * half_rows:(i + 1) * half_rows]
+
+                        @pl.when(x == i)
+                        def _():
+                            i_s[i * half_rows:(i + 1) * half_rows, k * V:(k + 1) * V] = jnp.concatenate(
+                                [half[start:start + size] for start, size in order], axis=0)
+
+                        @pl.when(x != i)
+                        def _():
+                            i_s[i * half_rows:(i + 1) * half_rows, k * V:(k + 1) * V] = half
                 else:
                     i_t[0, :, (k - Kr) * V:(k - Kr + 1) * V] = i_in[k].T
             if (q + 1) * per == Kr:
-                for g in range(len(groups)):
+                for g in range(len(slabs)):
                     row_i(g).start()
 
     cols = [side * m, side * m + 1, (1 - side) * (C - 1), 2 - side]
@@ -501,21 +506,27 @@
         def _():
             landed(az.at[s], zrecv.at[s])
 
-    def fill(d, u, spans, keep=None):
-        left = [i_t[d, at(start, size)] for start, size in spans]
-        left = left[0] if len(left) == 1 else jnp.concatenate(left, axis=0)
+    def product(d, u, start, size):
         right = [az[s].reshape(W, N) for s in pick(u)]
         right = right[0] if len(right) == 1 else jnp.concatenate(right, axis=1)
-        piece = lax.dot_general(left, right, (((1,), (0,)), ((), ())), preferred_element_type=jnp.float32)
+        return lax.dot_general(i_t[d, at(start, size)], right, (((1,), (0,)), ((), ())), preferred_element_type=jnp.float32)
+
+    def fill(d, u, start, size):
+        piece = product(d, u, start, size)
         for j, s in enumerate(pick(u)):
-            done = 0
-            for i, (start, size) in enumerate(spans):
-                part = piece[done:done + size, j * N:(j + 1) * N]
-                if keep is None:
-                    acc[d, s, at(start, size)] = part
-                else:
-                    keep[i, s] = part
-                done += size
+            acc[d, s, at(start, size)] = piece[:, j * N:(j + 1) * N]
+
+    def fill_both(part):
+        start, size = part
+        for u in (near, (2, 2)):
+            piece = product(1, u, mine + place[part], 2 * size)
+            for j, s in enumerate(pick(u)):
+                for i in range(2):
+                    one = piece[i * size:(i + 1) * size, j * N:(j + 1) * N]
+                    if part == final:
+                        last[i, s] = one
+                    else:
+                        acc[1, s, at(mine + i * rows + start, size, 8)] = one
 
     def from_to(u):
         return pl.ds(cols[u[0]], u[1]), pl.ds(u[0], u[1])
@@ -528,7 +539,7 @@
         give = 2 * (x if keep else 1 - x) + 1 - core
         for u in us:
             src, dst = from_to(u)
-            remote(acc.at[d, src, at(give * rows + start, size)], core_buf.at[d, min(keep, 1), dst, pl.ds(start, size)],
+            remote(acc.at[d, src, at(give * rows + start, size, 8)], core_buf.at[d, min(keep, 1), dst, pl.ds(start, size)],
                    csend, crecv.at[d, us[0][0] // 3, keep], layer=sib).start()
 
     def core_end(d, us, keep):
@@ -538,7 +549,7 @@
         landed(core_buf.at[d, min(keep, 1), slots, pl.ds(start, size)], crecv.at[d, us[0][0] // 3, keep])
         for u in us:
             src, dst = from_to(u)
-            acc[d, src, at(have * rows + start, size)] += core_buf[d, min(keep, 1), dst, start:start + size]
+            acc[d, src, at(have * rows + start, size, 8)] += core_buf[d, min(keep, 1), dst, start:start + size]
 
     def x_start(d, us):
         for u in us:
@@ -552,7 +563,7 @@
     def x_add(d, us, start, size, add=True):
         for u in us:
             src, dst = from_to(u)
-            where = at(l * rows + start, size)
+            where = at(l * rows + start, size, 8)
             if add:
                 acc[d, src, where] += x_buf[d, dst, start:start + size]
             else:
@@ -563,71 +574,66 @@
         sem = wrecv.at[d, jnp.where(slot == 0, 0, 1)]
         remote(acc.at[d, s, at(l * rows, size)], z_buf.at[d, slot, pl.ds(0, size)], wsend, sem, col=s).start()
 
-    def lean(d, s):
+    def lean(d, s, n):
         @pl.when(outer)
         def _():
-            remote(acc.at[d, s, at(l * rows, rows)], p_buf, wsend, precv, col=c ^ 1).start()
-
-    def across(d, s):
+            remote(acc.at[d, s, at(l * rows, rows)], p_buf.at[n], wsend, precv.at[n], col=c ^ 1).start()
+
+    def across(d, s, n):
         @pl.when(inner)
         def _():
-            landed(p_buf, precv)
-            acc[d, s, at(l * rows, rows)] += p_buf[...]
+            landed(p_buf.at[n], precv.at[n])
+            acc[d, s, at(l * rows, rows)] += p_buf[n]
             z_start(d, s)
 
     def hi_start(us):
         for u in us:
             for s in pick(u):
-                remote(acc.at[1, s, at(l * rows + lo, rows - lo)], hi_buf.at[c], hsend, hrecv.at[0], row=o, col=s).start()
-
-    def lo_start():
-        s = cols[3]
-        remote(acc.at[1, s, at(l * rows, lo)], lo_buf.at[lax.rem(c, m)], hsend, hrecv.at[1], row=o, col=s).start()
+                remote(acc.at[1, s, at(l * rows + lo, rows - lo, 8)], hi_buf.at[c], hsend, hrecv, row=o, col=s).start()
 
     most = (near, wide)
     for i in range(3):
         wait_piece(cols[i])
     for u in most:
-        fill(0, u, [(0, M)])
+        fill(0, u, 0, M)
     core_start(0, most, 0)
     core_start(0, most, 1)
     core_end(0, most, 0)
     x_start(0, most)
     core_end(0, most, 1)
 
-    slab_wait(0)
+    row_i(0).wait_recv()
     for u in most:
-        fill(1, u, [(other, half_rows)])
+        fill(1, u, other, half_rows)
     core_start(1, most, 0)
     x_wait(0, most)
     x_add(0, most, 0, rows)
     z_start(0, c ^ 1)
-    lean(0, cols[2])
+    lean(0, cols[2], 0)
     core_end(1, most, 0)
     x_start(1, most)
 
     wait_piece(cols[3])
-    fill(0, late, [(other, half_rows)])
+    fill(0, late, other, half_rows)
     core_start(0, [late], 0)
-    fill(1, late, [(other, half_rows)])
+    fill(1, late, other, half_rows)
     core_start(1, [late], 0)
-    across(0, cols[2])
+    across(0, cols[2], 0)
     core_end(0, [late], 0)
     x_start(0, [late])
     core_end(1, [late], 0)
     x_start(1, [late])
-    fill(0, late, [(mine, half_rows)])
+    fill(0, late, mine, half_rows)
     core_start(0, [late], 1)
 
-    slab_wait(1)
-    for u in (near, (2, 2)):
-        fill(1, u, both(first))
+    row_i(1).wait_recv()
+    fill_both(first)
     core_start(1, most, 1)
     core_start(1, [late], 1)
     core_end(0, [late], 1)
     x_wait(0, [late])
     x_add(0, [late], 0, rows)
-    z_start(0, cols[3])
+    lean(0, cols[3], 1)
     x_wait(1, most)
     core_end(1, most, 1)
     x_add(1, most, 0, T, add=False)
@@ -638,13 +644,24 @@
     x_wait(1, [late])
     x_add(1, [late], 0, T, add=False)
     x_add(1, [late], T, lo - T)
-    lo_start()
-
-    slab_wait(2)
-    for u in (near, (2, 2)):
-        fill(1, u, both(middle))
+    z_start(1, cols[3])
+
+    row_i(2).wait_recv()
+    fill_both(middle)
     core_start(1, most, 2)
     core_start(1, [late], 2)
+    def finish():
+        row_i(3).wait_recv()
+        fill_both(final)
+        for dc in range(C):
+            s = c ^ (C - 1 - dc)
+            for i in range(2):
+                remote(last.at[i, s], last_buf.at[core, c], lsend, lrecv, row=o, col=s, layer=2 * x + i).start()
+
+    @pl.when(core == 1)
+    def _():
+        finish()
+
     core_end(1, most, 2)
     x_add(1, most, lo, rows - lo)
     hi_start(most)
@@ -652,21 +669,15 @@
     x_add(1, [late], lo, rows - lo)
     hi_start([late])
 
-    slab_wait(3)
-    for u in (near, (2, 2)):
-        fill(1, u, both(final), keep=last)
-    for dc in range(C):
-        s = c ^ (C - 1 - dc)
-        for i in range(2):
-            remote(last.at[i, s], last_buf.at[core, c], lsend, lrecv, row=o, col=s, layer=2 * x + i).start()
-
+    @pl.when(core == 0)
+    def _():
+        finish()
+
+    across(0, cols[3], 1)
     landed(z_buf.at[1, 0, pl.ds(0, lo)], wrecv.at[1, 0])
-    y_out[...] = acc[1, c, at(l * rows, lo)] + z_buf[1, 0, :lo]
-
-    @pl.when(outer)
-    def _():
-        landed(z_buf.at[1, pl.ds(1, 2), pl.ds(0, lo)], wrecv.at[1, 1])
-        y_out[...] += z_buf[1, 1, :lo] + z_buf[1, 2, :lo]
+    y_sum = acc[1, c, at(l * rows, lo)] + z_buf[1, 0, :lo]
+    landed(z_buf.at[1, pl.ds(1, 2), pl.ds(0, lo)], wrecv.at[1, 1])
+    y_out[...] = y_sum + z_buf[1, 1, :lo] + z_buf[1, 2, :lo]
 
     remote(y_out, y_buf, ysend, yrecv, row=o).start()
 
@@ -679,19 +690,17 @@
     landed(z_buf.at[0, 0], wrecv.at[0, 0])
     o_ref[...] = acc[0, c, at(l * rows, rows)] + z_buf[0, 0]
 
+    landed(z_buf.at[0, 0], wrecv.at[0, 1])
+
     @pl.when(outer)
     def _():
-        landed(z_buf.at[0, 0], wrecv.at[0, 1])
         o_ref[...] += z_buf[0, 1]
 
     @pl.when(inner)
     def _():
-        landed(z_buf.at[0, pl.ds(1, 2)], wrecv.at[0, 1])
-        o_ref[...] += z_buf[0, 1] + z_buf[0, 2]
-        landed(lo_buf, hrecv.at[1])
-        o_ref[:lo] += lo_buf[0] + lo_buf[1]
-
-    landed(hi_buf, hrecv.at[0])
+        o_ref[...] += z_buf[0, 2]
+
+    landed(hi_buf, hrecv)
     high = o_ref[lo:]
     for s in range(C):
         high += hi_buf[s]
@@ -705,9 +714,8 @@
     landed(y_buf, yrecv)
     o_ref[:lo] += y_buf[...]
 
-    landed(acc.at[0, 0, pl.ds(0, 3 * rows + 2 * lo)] if 3 * rows + 2 * lo <= M else acc.at[0, pl.ds(0, 2), pl.ds(0, (3 * rows + 2 * lo) // 2)],
-           wsend)
-    landed(acc.at[0, 0, pl.ds(0, C * (rows - lo) + lo)], hsend)
+    landed(acc.at[0, pl.ds(0, m), pl.ds(0, 3 * (rows + lo) // m)], wsend)
+    landed(hi_buf, hsend)
     landed(last, lsend)
     landed(y_out, ysend)
 
@@ -718,8 +726,8 @@
     rows = M // L
     Kr = K // R
     m = C // R
-    T = 16
-    lo = rows * 5 // 6 // 16 * 16
+    T = 8
+    lo = 72
     dma = pltpu.SemaphoreType.DMA
     f32, bf16 = jnp.float32, jnp.bfloat16
     anyspace = pl.BlockSpec(memory_space=pl.ANY)
@@ -738,23 +746,22 @@
             pltpu.VMEM((2, C, T, N), f32),
             pltpu.VMEM((2, 2, C, rows, N), f32),
             pltpu.VMEM((2, C, rows, N), f32),
-            pltpu.VMEM((rows, N), f32),
+            pltpu.VMEM((2, rows, N), f32),
             pltpu.VMEM((2, C - 1, rows, N), f32),
             pltpu.VMEM((lo, N), f32),
             pltpu.VMEM((lo, N), f32),
             pltpu.VMEM((2, C, T, N), f32),
             pltpu.VMEM((C, rows - lo, N), f32),
-            pltpu.VMEM((m, lo, N), f32),
             dma, dma((Kr,)),
             dma, dma((Kr, m)),
             dma, dma((4,)),
             dma, dma((C,)),
             dma, dma((2, 2, 3)),
             dma, dma((2, 2)),
-            dma, dma, dma((2, 2)),
+            dma, dma((2,)), dma((2, 2)),
             dma, dma,
             dma, dma,
-            dma, dma((2,)),
+            dma, dma,
             pltpu.SemaphoreType.REGULAR((2, C - 2)),
         ],
         compiler_params=pltpu.CompilerParams(collective_id=0, has_side_effects=True),

time: 69.8 us -> 68.5 us (0.981)
  Pallas kernels: 68.8 us -> 67.6 us
    pallas_call x1, Pallas kernels: 68.8 us -> 67.6 us  [swift_call(): pl.pallas_call(functools.partial(swift, R, C, L, T, lo), out_shape=pltpu....]
where the time goes in v5:
time: 68.5 us; the launch traced here: 68.3 us
  Pallas kernels  67.6 us (99%)
  other arithmetic  0.71 us (1%)
    pallas_call x1, Pallas kernels, swift_call(): pl.pallas_call(functools.partial(swift, R, C, L, T, lo), out_shape=pltpu....  67.6 us

profile of v5, /device:TPU:0, one launch (start us, length us, event | category | flops | bytes accessed | tf_op | source)
XLA Modules:
  0.0 68.3 jit_solution(2795408752603897124)
XLA Ops:
  0.0 0.0 copy-start.1
  0.0 0.0 copy-start.2
  0.0 0.0 copy-start
  0.0 67.6 %shard_map.55 = f32[96,128]{1,0:T(8,128)S(1)} custom-call(bf16[16,256,384]{2,1,0:T(8,128)(2,1)} %i_ref.1, bf16[16,512,128]{2,1,0:T(8,128)(2,1)} %a_ref.1), custom_call_target="tpu_custom_call" | custom-call | tf_op jit(solution)/shard_map/pallas_call | solution.py:734
  67.6 0.0 copy-done.1
  67.6 0.0 copy-done.2
  67.6 0.0 copy-done
  67.6 0.7 %add_divide_fusion = f32[96,128]{1,0:T(8,128)} fusion(f32[96,128]{1,0:T(8,128)S(1)} %shard_map.55, bf16[96,128]{1,0:T(8,128)(2,1)S(1)} %copy-done, f32[128]{0:T(128)S(1)} %copy-done.1, f32[96]{0:T(128)S(1)} %copy-done.2), kind=kLoop, calls=%fused_computation | loop fusion | flops 49152 | bytes 123776 | tf_op jit(solution)/shard_map/div | solution.py:776
Async XLA Ops:
  0.0 67.6 %copy-start.1 = (f32[128]{0:T(128)S(1)}, f32[128]{0:T(128)}, u32[]{:S(2)}) copy-start(f32[128]{0:T(128)} %param.9) | copy-start | bytes 1540
  0.0 67.6 %copy-start.2 = (f32[96]{0:T(128)S(1)}, f32[96]{0:T(128)}, u32[]{:S(2)}) copy-start(f32[96]{0:T(128)} %param.8) | copy-start | bytes 1156
  0.0 67.6 %copy-start = (bf16[96,128]{1,0:T(8,128)(2,1)S(1)}, bf16[96,128]{1,0:T(8,128)(2,1)}, u32[]{:S(2)}) copy-start(bf16[96,128]{1,0:T(8,128)(2,1)} %param.7) | copy-start | bytes 73732

commit v6 on v5

--- a/solution.py
+++ b/solution.py
@@ -358,11 +358,18 @@
 
     def row_a(q, j):
         span = pl.ds(j * V, V)
-        return remote(a_ref.at[o * Kr + q, span], a_x.at[q, span], asend, arecv.at[q, j], row=o)
-
-    for q in range(Kr):
-        for j in range(m):
-            row_a(q, j).start()
+        return remote(a_ref.at[o * Kr + q, span], a_x.at[q, span], asend, arecv.at[j if q == 0 else q + m - 1], row=o)
+
+    def row_start(*qs):
+        for q in qs:
+            for j in range(m):
+                row_a(q, j).start()
+
+    row_start(*range(2))
+
+    @pl.when(core == 0)
+    def _():
+        row_start(*range(2, Kr))
 
     def col_start(d, *qs, js=range(m)):
         for q in qs:
@@ -402,6 +409,10 @@
         def _():
             pl.semaphore_wait(there.at[1, t - 2], 1)
 
+    @pl.when(core == 1)
+    def _():
+        row_start(*range(2, Kr))
+
     @pl.when(away)
     def _():
         col_start(0, *range(hold))
@@ -443,7 +454,10 @@
 
     for q in range(Kr):
         for j in range(m):
-            row_a(q, j).wait_recv()
+            if q == 0:
+                row_a(q, j).wait_recv()
+            elif j == 0:
+                landed(a_x.at[q], arecv.at[q + m - 1])
             if hold <= q < turnover:
                 @pl.when(outer | away)
                 def _():
@@ -727,7 +741,7 @@
     Kr = K // R
     m = C // R
     T = 8
-    lo = 72
+    lo = rows * 3 // 4 // 8 * 8
     dma = pltpu.SemaphoreType.DMA
     f32, bf16 = jnp.float32, jnp.bfloat16
     anyspace = pl.BlockSpec(memory_space=pl.ANY)
@@ -753,7 +767,7 @@
             pltpu.VMEM((2, C, T, N), f32),
             pltpu.VMEM((C, rows - lo, N), f32),
             dma, dma((Kr,)),
-            dma, dma((Kr, m)),
+            dma, dma((Kr + m - 1,)),
             dma, dma((4,)),
             dma, dma((C,)),
             dma, dma((2, 2, 3)),
@@ -769,7 +783,9 @@
 
 
 def local(R, C, L, integrals, amplitudes, coulomb, row_gap, col_gap):
-    swift_fits = R == 2 and C == 4 and L == 4 and integrals.shape[2] % (16 * L) == 0
+    K, V, M = integrals.shape
+    N = amplitudes.shape[2]
+    swift_fits = (R, C, L) == (2, 4, 4) and K % 16 == 0 and M % (16 * L) == 0 and V % 128 == 0 and N % 128 == 0
     call = swift_call if swift_fits else general_call
     own_rows = call(R, C, L, integrals, amplitudes)
     gap_sum = row_gap[:, None] + col_gap[None, :]

time: 68.5 us -> 68.4 us (level)
  no operation moved by 1% of the time
where the time goes in v6:
time: 68.4 us; the launch traced here: 68.3 us
  Pallas kernels  67.5 us (99%)
  other arithmetic  0.71 us (1%)
    pallas_call x1, Pallas kernels, swift_call(): pl.pallas_call(functools.partial(swift, R, C, L, T, lo), out_shape=pltpu....  67.5 us

profile of v6, /device:TPU:0, one launch (start us, length us, event | category | flops | bytes accessed | tf_op | source)
XLA Modules:
  0.0 68.3 jit_solution(15875114545023281781)
XLA Ops:
  0.0 0.0 copy-start.1
  0.0 0.0 copy-start.2
  0.0 0.0 copy-start
  0.0 67.5 %shard_map.55 = f32[96,128]{1,0:T(8,128)S(1)} custom-call(bf16[16,256,384]{2,1,0:T(8,128)(2,1)} %i_ref.1, bf16[16,512,128]{2,1,0:T(8,128)(2,1)} %a_ref.1), custom_call_target="tpu_custom_call" | custom-call | tf_op jit(solution)/shard_map/pallas_call | solution.py:748
  67.5 0.0 copy-done.1
  67.6 0.0 copy-done.2
  67.6 0.0 copy-done
  67.6 0.7 %add_divide_fusion = f32[96,128]{1,0:T(8,128)} fusion(f32[96,128]{1,0:T(8,128)S(1)} %shard_map.55, bf16[96,128]{1,0:T(8,128)(2,1)S(1)} %copy-done, f32[128]{0:T(128)S(1)} %copy-done.1, f32[96]{0:T(128)S(1)} %copy-done.2), kind=kLoop, calls=%fused_computation | loop fusion | flops 49152 | bytes 123776 | tf_op jit(solution)/shard_map/div | solution.py:792
Async XLA Ops:
  0.0 67.5 %copy-start.1 = (f32[128]{0:T(128)S(1)}, f32[128]{0:T(128)}, u32[]{:S(2)}) copy-start(f32[128]{0:T(128)} %param.9) | copy-start | bytes 1540
  0.0 67.6 %copy-start.2 = (f32[96]{0:T(128)S(1)}, f32[96]{0:T(128)}, u32[]{:S(2)}) copy-start(f32[96]{0:T(128)} %param.8) | copy-start | bytes 1156
  0.0 67.6 %copy-start = (bf16[96,128]{1,0:T(8,128)(2,1)S(1)}, bf16[96,128]{1,0:T(8,128)(2,1)}, u32[]{:S(2)}) copy-start(bf16[96,128]{1,0:T(8,128)(2,1)} %param.7) | copy-start | bytes 73732

commit v7 on v6

--- a/solution.py
+++ b/solution.py
@@ -302,7 +302,8 @@
     )(integrals, amplitudes)
 
 
-def swift(R, C, L, T, lo, i_ref, a_ref, o_ref,
+def swift(R, C, L, T, lo, i_ref, a_ref, b_ref, rg_ref, cg_ref, o_ref,
+          bare, gap_r, gap_c, gap, gsem,
           a_x, az, i_in, i_s, i_t, acc, last, core_buf, x_buf, p_buf, z_buf, y_out, y_buf, last_buf, hi_buf,
           own, iown, asend, arecv, isend, irecv, zsend, zrecv,
           csend, crecv, xsend, xrecv, wsend, precv, wrecv, ysend, yrecv, lsend, lrecv, hsend, hrecv, there):
@@ -430,6 +431,9 @@
 
     def own_k(n):
         return (r if n * per >= Kr else o) * Kr + n * per % Kr
+
+    for n, (src, dst) in enumerate(((b_ref, bare), (rg_ref, gap_r), (cg_ref, gap_c))):
+        pltpu.make_async_copy(src, dst, gsem.at[n]).start()
 
     for n in range(K // per):
         pltpu.make_async_copy(i_ref.at[pl.ds(own_k(n), per)], i_in.at[pl.ds(n * per, per)], iown.at[n]).start()
@@ -695,6 +699,9 @@
 
     remote(y_out, y_buf, ysend, yrecv, row=o).start()
 
+    for n, (src, dst) in enumerate(((b_ref, bare), (rg_ref, gap_r), (cg_ref, gap_c))):
+        pltpu.make_async_copy(src, dst, gsem.at[n]).wait()
+    gap[...] = jnp.broadcast_to(gap_r[...], (N, rows)).T + gap_c[...]
     landed(a_x, asend)
     landed(az.at[pl.ds(0, m + 1)], zsend)
     landed(i_s, isend)
@@ -702,7 +709,7 @@
     landed(acc.at[0, :, pl.ds(0, half_rows)], xsend)
 
     landed(z_buf.at[0, 0], wrecv.at[0, 0])
-    o_ref[...] = acc[0, c, at(l * rows, rows)] + z_buf[0, 0]
+    o_ref[...] = bare[...].astype(jnp.float32) + acc[0, c, at(l * rows, rows)] + z_buf[0, 0]
 
     landed(z_buf.at[0, 0], wrecv.at[0, 1])
 
@@ -727,6 +734,7 @@
     o_ref[:T] = tail
     landed(y_buf, yrecv)
     o_ref[:lo] += y_buf[...]
+    o_ref[...] = o_ref[...] / gap[...]
 
     landed(acc.at[0, pl.ds(0, m), pl.ds(0, 3 * (rows + lo) // m)], wsend)
     landed(hi_buf, hsend)
@@ -734,7 +742,7 @@
     landed(y_out, ysend)
 
 
-def swift_call(R, C, L, integrals, amplitudes):
+def swift_call(R, C, L, integrals, amplitudes, coulomb, row_gap, col_gap):
     K, V, M = integrals.shape
     V_row, N = amplitudes.shape[1:]
     rows = M // L
@@ -748,9 +756,10 @@
     return pl.pallas_call(
         functools.partial(swift, R, C, L, T, lo),
         out_shape=pltpu.VMEM((rows, N), f32),
-        in_specs=[anyspace, anyspace],
+        in_specs=[anyspace] * 5,
         out_specs=pl.BlockSpec(memory_space=pltpu.VMEM),
         scratch_shapes=[
+            pltpu.VMEM((rows, N), bf16), pltpu.VMEM((1, rows), f32), pltpu.VMEM((1, N), f32), pltpu.VMEM((rows, N), f32), dma((3,)),
             pltpu.VMEM((Kr, V_row, N), bf16),
             pltpu.VMEM((C, Kr, V, N), bf16),
             pltpu.VMEM((K, V, M), bf16),
@@ -779,15 +788,16 @@
             pltpu.SemaphoreType.REGULAR((2, C - 2)),
         ],
         compiler_params=pltpu.CompilerParams(collective_id=0, has_side_effects=True),
-    )(integrals, amplitudes)
+    )(integrals, amplitudes, coulomb, row_gap[None, :], col_gap[None, :])
 
 
 def local(R, C, L, integrals, amplitudes, coulomb, row_gap, col_gap):
     K, V, M = integrals.shape
     N = amplitudes.shape[2]
     swift_fits = (R, C, L) == (2, 4, 4) and K % 16 == 0 and M % (16 * L) == 0 and V % 128 == 0 and N % 128 == 0
-    call = swift_call if swift_fits else general_call
-    own_rows = call(R, C, L, integrals, amplitudes)
+    if swift_fits:
+        return swift_call(R, C, L, integrals, amplitudes, coulomb, row_gap, col_gap)
+    own_rows = general_call(R, C, L, integrals, amplitudes)
     gap_sum = row_gap[:, None] + col_gap[None, :]
     return (coulomb.astype(jnp.float32) + own_rows) / gap_sum
 

time: 68.4 us -> 68.3 us (level)
  other arithmetic: 0.71 us -> 0 us
    div x1 -> x0, other arithmetic: 0.71 us -> none  [local(): return (coulomb.astype(jnp.float32) + own_rows) / gap_sum]
where the time goes in v7:
time: 68.3 us; the launch traced here: 68.1 us
  Pallas kernels  67.5 us (99%)
    pallas_call x1, Pallas kernels, swift_call(): pl.pallas_call(functools.partial(swift, R, C, L, T, lo), out_shape=pltpu....  67.5 us

profile of v7, /device:TPU:0, one launch (start us, length us, event | category | flops | bytes accessed | tf_op | source)
XLA Modules:
  0.0 68.1 jit_solution(9030633401341260091)
XLA Ops:
  0.0 67.5 %shard_map.55 = f32[96,128]{1,0:T(8,128)S(1)} custom-call(bf16[16,256,384]{2,1,0:T(8,128)(2,1)} %i_ref.1, bf16[16,512,128]{2,1,0:T(8,128)(2,1)} %a_ref.1, bf16[96,128]{1,0:T(8,128)(2,1)} %b_ref.1, f32[1,96]{1,0:T(1,128)} %bitcast.2, f32[1,128]{1,0:T(1,128)} %bitcast.3), custom_call_target="tpu_custom_call" | custom-call | tf_op jit(solution)/shard_map/pallas_call | solution.py:756
  67.5 0.6 copy.7

commit v8 on v7

--- a/solution.py
+++ b/solution.py
@@ -383,7 +383,7 @@
                 def _():
                     remote(src, az.at[c, q], zsend, zrecv.at[c], col=b).start()
 
-    ahead, hold, turnover = 3, 2, Kr - 2
+    ahead, hold, turnover = 2, 3, Kr - 3
 
     @pl.when(home)
     def _():
@@ -749,7 +749,7 @@
     Kr = K // R
     m = C // R
     T = 8
-    lo = rows * 3 // 4 // 8 * 8
+    lo = rows * 2 // 3 // 8 * 8
     dma = pltpu.SemaphoreType.DMA
     f32, bf16 = jnp.float32, jnp.bfloat16
     anyspace = pl.BlockSpec(memory_space=pl.ANY)

time: 68.3 us -> 68.3 us (level)
  no operation moved by 1% of the time
where the time goes in v8:
time: 68.3 us; the launch traced here: 68.1 us
  Pallas kernels  67.5 us (99%)
    pallas_call x1, Pallas kernels, swift_call(): pl.pallas_call(functools.partial(swift, R, C, L, T, lo), out_shape=pltpu....  67.5 us

profile of v8, /device:TPU:0, one launch (start us, length us, event | category | flops | bytes accessed | tf_op | source)
XLA Modules:
  0.0 68.1 jit_solution(10613557579587464557)
XLA Ops:
  0.0 67.5 %shard_map.55 = f32[96,128]{1,0:T(8,128)S(1)} custom-call(bf16[16,256,384]{2,1,0:T(8,128)(2,1)} %i_ref.1, bf16[16,512,128]{2,1,0:T(8,128)(2,1)} %a_ref.1, bf16[96,128]{1,0:T(8,128)(2,1)} %b_ref.1, f32[1,96]{1,0:T(1,128)} %bitcast.2, f32[1,128]{1,0:T(1,128)} %bitcast.3), custom_call_target="tpu_custom_call" | custom-call | tf_op jit(solution)/shard_map/pallas_call | solution.py:756
  67.5 0.6 copy.7
